TPU v7x, 256 devices: a whole 4x4x8 slice. The times are simulated.
256 devices in a mesh: seq: 32 (over x_hi, z, core), batch: 8 (over x_lo, y).
Axes of the slice: x: 4 (x_hi: 2, x_lo: 2; x = x_hi * 2 + x_lo), y: 4, z: 8, core: 2. Of those that a mesh axis runs over, the one named last changes fastest.
Arguments:
- bases: int32 [65536, 128], P(('batch', 'seq')), parts along dimension 0, may hold values from 0 to 3
- embed_table: bfloat16 [512, 768], replicated, may hold values from -0.5 to 0.5
- norm_gains: float32 [3, 768], replicated, may hold values from 0.1 to 1.9
- depth_taps: float32 [3, 5, 768], replicated, may hold values from -2.5 to 2.5
- point_weight: bfloat16 [3, 768, 768], replicated, may hold values from -0.21875 to 0.21875
- query_weight: bfloat16 [768, 128], replicated, may hold values from -0.5390625 to 0.5390625
- key_weight: bfloat16 [768, 128], replicated, may hold values from -0.5390625 to 0.5390625
- pair_kernel: bfloat16 [3, 3, 128, 128], replicated, may hold values from -0.1875 to 0.1875
Outputs:
- trunk: bfloat16 [65536, 768], P(('batch', 'seq')), parts along dimension 0
- pair_map: bfloat16 [4096, 512, 128], P(('batch', 'seq')), parts along dimension 0
There are 8 independent parts, one for each index of `batch`. A program takes and returns all parts, laid end to end along the dimension named above; an argument that names none is the same for every part. Nothing has to cross between parts.
All inputs are finite; a program needn't handle non-finite values.
Results may differ from a plain program's by a relative error of at most 0.018.
Values may be sent and summed in bfloat16 or wider, within the bound.
No kernel may reach another device: no remote copies, remote signals or barrier semaphores. Data moves between devices by JAX's collectives and lax.ppermute only.
A program may use at most 64 MiB of HBM per device.

v0:
```python
import jax
import jax.numpy as jnp
from jax import lax
from jax.sharding import PartitionSpec as P

KW = 5
FIRST_DILATION = 2
SECOND_DILATION = 8
THIRD_DILATION = 32
POOL = 16


def with_halo(cells, sides, width):
    for axis, dim in sides:
        count = lax.axis_size(axis)
        ends = count - 1
        head = lax.slice_in_dim(cells, 0, width, axis=dim)
        tail = lax.slice_in_dim(cells, cells.shape[dim] - width, cells.shape[dim], axis=dim)
        cells = jnp.concatenate(
            [
                lax.ppermute(tail, axis, [(i, (i + 1) % count) for i in range(ends)]),
                cells,
                lax.ppermute(head, axis, [((i + 1) % count, i) for i in range(ends)]),
            ],
            axis=dim,
        )
    return cells


def embed_bases(bases, embed_table):
    one_hot_bases = (bases[:, :, None] == jnp.arange(4, dtype=jnp.int32)).astype(jnp.bfloat16)
    one_hot_bases = one_hot_bases.reshape(bases.shape[0], -1)
    return jnp.dot(one_hot_bases, embed_table, preferred_element_type=jnp.float32).astype(
        jnp.bfloat16
    )


def normalize(value_rows, gain):
    floats = value_rows.astype(jnp.float32)
    scale = lax.rsqrt(jnp.mean(floats * floats, axis=-1, keepdims=True) + 1e-06)
    return (floats * scale * gain).astype(jnp.bfloat16)


def mix_rows(inner, normed, taps, point, dilation_reach, rows):
    summed = jnp.zeros((rows, normed.shape[1]), jnp.float32)
    for offset in range(KW):
        summed = (
            summed
            + normed[offset * dilation_reach : offset * dilation_reach + rows].astype(jnp.float32)
            * taps[offset]
        )
    activated = jax.nn.gelu(summed).astype(jnp.bfloat16)
    return (
        inner.astype(jnp.float32) + jnp.dot(activated, point, preferred_element_type=jnp.float32)
    ).astype(jnp.bfloat16)


def pair_conv(extended, pair_kernel, rows, width):
    padded = jnp.pad(extended, ((0, 0), (1, 1), (0, 0)))
    channels = extended.shape[2]
    summed = jnp.zeros((rows * width, channels), jnp.float32)
    for row_tap in range(3):
        for col_tap in range(3):
            window = padded[row_tap : row_tap + rows, col_tap : col_tap + width].reshape(
                rows * width, channels
            )
            summed = summed + jnp.dot(
                window, pair_kernel[row_tap, col_tap], preferred_element_type=jnp.float32
            )
    center = extended[1 : rows + 1].astype(jnp.float32).reshape(rows * width, channels)
    return (center + jax.nn.gelu(summed)).astype(jnp.bfloat16).reshape(rows, width, channels)


def on_device(
    bases, embed_table, norm_gains, depth_taps, point_weight, query_weight, key_weight, pair_kernel
):
    dilation_reaches = (FIRST_DILATION, SECOND_DILATION, THIRD_DILATION)
    current = embed_bases(bases, embed_table)
    slab_rows = current.shape[0]
    for trunk_layer in range(3):
        dilation_reach = dilation_reaches[trunk_layer]
        normed = normalize(current, norm_gains[trunk_layer])
        widened = with_halo(normed, (("seq", 0),), 2 * dilation_reach)
        current = mix_rows(
            current,
            widened,
            depth_taps[trunk_layer],
            point_weight[trunk_layer],
            dilation_reach,
            slab_rows,
        )
    pooled = jnp.mean(
        current.astype(jnp.float32).reshape(-1, POOL, current.shape[1]), axis=1
    ).astype(jnp.bfloat16)
    queries = jnp.dot(pooled, query_weight, preferred_element_type=jnp.float32).astype(jnp.bfloat16)
    all_keys = jnp.dot(
        lax.all_gather(pooled, "seq", axis=0, tiled=True),
        key_weight,
        preferred_element_type=jnp.float32,
    ).astype(jnp.bfloat16)
    key_floats = all_keys.astype(jnp.float32)[None, :, :]
    pair_rows = queries.shape[0]
    pair = (queries.astype(jnp.float32)[:, None, :] * key_floats).astype(jnp.bfloat16)
    extended = with_halo(pair, (("seq", 0),), 1)
    pair_map = pair_conv(extended, pair_kernel, pair_rows, all_keys.shape[0])
    return (current, pair_map)


def solution(mesh):
    return jax.shard_map(
        on_device,
        mesh=mesh,
        in_specs=(P(("batch", "seq"), None), P(), P(), P(), P(), P(), P(), P()),
        out_specs=(P(("batch", "seq"), None), P(("batch", "seq"), None, None)),
        check_vma=False,
    )
```

profile of v0, /device:TPU:14, one launch (start us, length us, event | category | flops | bytes accessed | tf_op | source)
XLA Modules:
  0.0 109.2 jit_solution(7016129010796559855)
XLA Ops:
  0.6 0.0 copy-start
  0.6 0.8 slice_reduce_fusion.5
  1.5 0.1 eq.23
  1.6 1.0 copy.10
  2.6 0.0 copy-start.5
  2.6 0.1 eq.20
  2.7 0.2 eq.21
  2.9 0.0 copy-done
  2.9 0.7 multiply_reduce_fusion.2
  3.6 0.1 multiply_convert_fusion.3
  3.8 1.9 %collective-permute-start = (bf16[4,768]{1,0:T(4,128)(2,1)S(1)}, bf16[4,768]{1,0:T(4,128)(2,1)S(1)}, u32[]{:S(2)}, u32[]{:S(2)}) collective-permute-start(bf16[4,768]{1,0:T(4,128)(2,1)S(1)} %get-tuple-element.34), channel_id=1, source_target_pairs={{0,8},{8,16},{16,24},{24,32},{32,40},{40,48},{48,56},{56,64},{64,7... | collective-permute-start | bytes 18440 | tf_op jit(solution)/shard_map/ppermute | solution.py:21
  5.7 8.0 %collective-permute-start.1 = (bf16[4,768]{1,0:T(4,128)(2,1)S(1)}, bf16[4,768]{1,0:T(4,128)(2,1)S(1)}, u32[]{:S(2)}, u32[]{:S(2)}) collective-permute-start(bf16[4,768]{1,0:T(4,128)(2,1)S(1)} %get-tuple-element.35), channel_id=1, source_target_pairs={{8,0},{16,8},{24,16},{32,24},{40,32},{48,40},{56,48},{64,56},{72,6... | collective-permute-start | bytes 18440 | tf_op jit(solution)/shard_map/ppermute | solution.py:23
  13.8 0.0 copy-done.5
  13.8 0.1 slice_reduce_fusion.4
  13.9 0.0 collective-permute-done
  13.9 1.2 %collective-permute-done.1 = bf16[4,768]{1,0:T(4,128)(2,1)S(1)} collective-permute-done((bf16[4,768]{1,0:T(4,128)(2,1)S(1)}, bf16[4,768]{1,0:T(4,128)(2,1)S(1)}, u32[]{:S(2)}, u32[]{:S(2)}) %collective-permute-start.1) | collective-permute-done | bytes 6176 | tf_op jit(solution)/shard_map/ppermute | solution.py:23
  15.1 0.0 copy-start.6
  15.1 2.6 %multiply_reduce_fusion.1 = (f32[256]{0:T(256)S(1)}, f32[256,768]{1,0:T(8,128)S(1)}) fusion(f32[256,768]{1,0:T(8,128)S(1)} %get-tuple-element.37, bf16[3,768,768]{2,1,0:T(8,128)(2,1)} %param.12, bf16[256,768]{1,0:T(8,128)(2,1)S(1)} %multiply_convert_fusion.3, bf16[4,768]{1,0:T(4,128)(2,1)S(1)} %collective-permute-done.1, ...), kind=kOutput, calls=%fused_computation.80 | convolution fusion | flops 309853952 | bytes 3174400 | tf_op jit(solution)/shard_map/dot_general | solution.py:54
  17.7 0.1 multiply_convert_fusion.2
  17.9 1.9 %collective-permute-start.2 = (bf16[16,768]{1,0:T(8,128)(2,1)S(1)}, bf16[16,768]{1,0:T(8,128)(2,1)S(1)}, u32[]{:S(2)}, u32[]{:S(2)}) collective-permute-start(bf16[16,768]{1,0:T(8,128)(2,1)S(1)} %get-tuple-element.32), channel_id=1, source_target_pairs={{0,8},{8,16},{16,24},{24,32},{32,40},{40,48},{48,56},{56,64},{64,7... | collective-permute-start | bytes 73736 | tf_op jit(solution)/shard_map/ppermute | solution.py:21
  19.8 7.3 %collective-permute-start.3 = (bf16[16,768]{1,0:T(8,128)(2,1)S(1)}, bf16[16,768]{1,0:T(8,128)(2,1)S(1)}, u32[]{:S(2)}, u32[]{:S(2)}) collective-permute-start(bf16[16,768]{1,0:T(8,128)(2,1)S(1)} %get-tuple-element.33), channel_id=1, source_target_pairs={{8,0},{16,8},{24,16},{32,24},{40,32},{48,40},{56,48},{64,56},{72,6... | collective-permute-start | bytes 73736 | tf_op jit(solution)/shard_map/ppermute | solution.py:23
  27.0 0.0 collective-permute-done.2
  27.1 1.5 %collective-permute-done.3 = bf16[16,768]{1,0:T(8,128)(2,1)S(1)} collective-permute-done((bf16[16,768]{1,0:T(8,128)(2,1)S(1)}, bf16[16,768]{1,0:T(8,128)(2,1)S(1)}, u32[]{:S(2)}, u32[]{:S(2)}) %collective-permute-start.3) | collective-permute-done | bytes 24608 | tf_op jit(solution)/shard_map/ppermute | solution.py:23
  28.5 0.0 copy-done.6
  28.6 1.0 multiply_reduce_fusion
  29.5 0.1 multiply_convert_fusion.1
  29.7 1.9 %collective-permute-start.4 = (bf16[64,768]{1,0:T(8,128)(2,1)S(1)}, bf16[64,768]{1,0:T(8,128)(2,1)S(1)}, u32[]{:S(2)}, u32[]{:S(2)}) collective-permute-start(bf16[64,768]{1,0:T(8,128)(2,1)S(1)} %get-tuple-element.30), channel_id=1, source_target_pairs={{0,8},{8,16},{16,24},{24,32},{32,40},{40,48},{48,56},{56,64},{64,7... | collective-permute-start | bytes 294920 | tf_op jit(solution)/shard_map/ppermute | solution.py:21
  31.6 7.3 %collective-permute-start.5 = (bf16[64,768]{1,0:T(8,128)(2,1)S(1)}, bf16[64,768]{1,0:T(8,128)(2,1)S(1)}, u32[]{:S(2)}, u32[]{:S(2)}) collective-permute-start(bf16[64,768]{1,0:T(8,128)(2,1)S(1)} %get-tuple-element.31), channel_id=1, source_target_pairs={{8,0},{16,8},{24,16},{32,24},{40,32},{48,40},{56,48},{64,56},{72,6... | collective-permute-start | bytes 294920 | tf_op jit(solution)/shard_map/ppermute | solution.py:23
  38.9 0.4 collective-permute-done.4
  39.3 1.8 %collective-permute-done.5 = bf16[64,768]{1,0:T(8,128)(2,1)S(1)} collective-permute-done((bf16[64,768]{1,0:T(8,128)(2,1)S(1)}, bf16[64,768]{1,0:T(8,128)(2,1)S(1)}, u32[]{:S(2)}, u32[]{:S(2)}) %collective-permute-start.5) | collective-permute-done | bytes 98336 | tf_op jit(solution)/shard_map/ppermute | solution.py:23
  41.1 0.0 copy-start.4
  41.1 0.0 copy-start.3
  41.1 1.8 %convert_reduce_fusion = (f32[16,768]{1,0:T(8,128)S(1)}, bf16[256,768]{1,0:T(8,128)(2,1)}) fusion(f32[256,768]{1,0:T(8,128)S(1)} %get-tuple-element.41, bf16[3,768,768]{2,1,0:T(8,128)(2,1)S(1)} %copy-done.6, bf16[256,768]{1,0:T(8,128)(2,1)S(1)} %multiply_convert_fusion.1, bf16[64,768]{1,0:T(8,128)(2,1)S(1)} %collective-permute-done.5, ...), kind=kOutput, calls=%fused_computation.76 | convolution fusion | flops 309645312 | bytes 3018752 | tf_op jit(solution)/shard_map/dot_general | solution.py:54
  42.9 39.0 %all_gather.3 = bf16[512,768]{1,0:T(8,128)(2,1)S(1)} all-gather(bf16[16,768]{1,0:T(8,128)(2,1)S(1)} %multiply_convert_fusion.4), channel_id=1, replica_groups=mesh['seq'=32,'batch'=8] {'seq'}, dimensions={0}, use_global_device_ids=true | all-gather | bytes 811008 | tf_op jit(solution)/shard_map/all_gather | solution.py:97
  81.9 0.0 copy-done.4
  81.9 0.1 fusion.29
  82.0 0.0 copy-done.3
  82.0 0.4 fusion.28
  82.4 0.5 multiply_convert_fusion
  82.9 2.3 %collective-permute-start.6 = (bf16[1,512,128]{2,1,0:T(8,128)(2,1)S(1)}, bf16[1,512,128]{2,1,0:T(8,128)(2,1)S(1)}, u32[]{:S(2)}, u32[]{:S(2)}) collective-permute-start(bf16[1,512,128]{2,1,0:T(8,128)(2,1)S(1)} %get-tuple-element.28), channel_id=1, source_target_pairs={{0,8},{8,16},{16,24},{24,32},{32,40},{40,48},{48,56},{56,64},{64,7... | collective-permute-start | bytes 393224 | tf_op jit(solution)/shard_map/ppermute | solution.py:21
  85.2 7.1 %collective-permute-start.7 = (bf16[1,512,128]{2,1,0:T(8,128)(2,1)S(1)}, bf16[1,512,128]{2,1,0:T(8,128)(2,1)S(1)}, u32[]{:S(2)}, u32[]{:S(2)}) collective-permute-start(bf16[1,512,128]{2,1,0:T(8,128)(2,1)S(1)} %get-tuple-element.29), channel_id=1, source_target_pairs={{8,0},{16,8},{24,16},{32,24},{40,32},{48,40},{56,48},{64,56},{72,6... | collective-permute-start | bytes 393224 | tf_op jit(solution)/shard_map/ppermute | solution.py:23
  92.3 0.5 collective-permute-done.6
  92.8 1.8 %collective-permute-done.7 = bf16[1,512,128]{2,1,0:T(8,128)(2,1)S(1)} collective-permute-done((bf16[1,512,128]{2,1,0:T(8,128)(2,1)S(1)}, bf16[1,512,128]{2,1,0:T(8,128)(2,1)S(1)}, u32[]{:S(2)}, u32[]{:S(2)}) %collective-permute-start.7) | collective-permute-done | bytes 131104 | tf_op jit(solution)/shard_map/ppermute | solution.py:23
  94.6 1.4 %fusion.15 = bf16[18,514,128]{2,1,0:T(8,128)(2,1)S(1)} fusion(bf16[1,512,128]{2,1,0:T(8,128)(2,1)S(1)} %collective-permute-done.7, bf16[16,512,128]{2,1,0:T(8,128)(2,1)S(1)} %multiply_convert_fusion, bf16[1,512,128]{2,1,0:T(8,128)(2,1)S(1)} %collective-permute-done.6), kind=kLoop, calls=%fused_computation.26 | loop fusion | flops 14211072 | bytes 4727808 | tf_op jit(solution)/shard_map/concatenate | solution.py:19
  96.1 0.0 copy-start.2
  96.1 3.8 %fusion.133 = (bf16[16,512,128]{2,1,0:T(8,128)(2,1)S(1)}, bf16[16,512,128]{2,1,0:T(8,128)(2,1)S(1)}, bf16[16,512,128]{2,1,0:T(8,128)(2,1)S(1)}, bf16[16,512,128]...) fusion(bf16[18,514,128]{2,1,0:T(8,128)(2,1)S(1)} %fusion.15), kind=kLoop, calls=%fused_computation.199 | loop fusion | bytes 25165824 | tf_op jit(solution)/shard_map/slice | solution.py:64
  99.9 0.0 copy-done.2
  99.9 0.7 fusion.107
  100.6 0.7 fusion.98
  101.3 0.4 pad_maximum_fusion
  101.6 0.7 convolution_add_fusion.6
  102.3 0.7 convolution_add_fusion.5
  103.0 0.7 convolution_add_fusion.4
  103.7 0.7 convolution_add_fusion.3
  104.4 0.7 convolution_add_fusion.2
  105.1 0.7 convolution_add_fusion.1
  105.8 0.0 copy-start.1
  105.8 3.3 %fusion.10 = bf16[8192,128]{1,0:T(8,128)(2,1)} fusion(f32[8192,128]{1,0:T(8,128)S(1)} %fusion.98, f32[8192,128]{1,0:T(8,128)S(1)} %convolution_add_fusion.1, bf16[8192,128]{1,0:T(8,128)(2,1)S(1)} %bitcast.80, bf16[8192,128]{1,0:T(8,128)(2,1)S(1)} %bitcast.72, bf16[3,3,128,128]{3,2,1,0:T(8,128)(2,1)S(1)} %copy-done.2), kind=kOutput, calls=%fused_computation.20 | convolution fusion | flops 282066944 | bytes 14712832 | tf_op jit(solution)/shard_map/dot_general | solution.py:67
  109.2 0.0 copy-done.1
  (9 shorter events, 0.1 us)
Async XLA Ops:
  0.6 2.3 %copy-start = (bf16[512,768]{1,0:T(8,128)(2,1)S(1)}, bf16[512,768]{1,0:T(8,128)(2,1)}, u32[]{:S(2)}) copy-start(bf16[512,768]{1,0:T(8,128)(2,1)} %param.9) | copy-start | bytes 2359300
  2.6 11.1 %copy-start.5 = (f32[3,5,768]{2,0,1:T(4,128)S(1)}, f32[3,5,768]{2,0,1:T(4,128)}, u32[]{:S(2)}) copy-start(f32[3,5,768]{2,0,1:T(4,128)} %param.11) | copy-start | bytes 138244
  3.8 10.1 %collective-permute-start = (bf16[4,768]{1,0:T(4,128)(2,1)S(1)}, bf16[4,768]{1,0:T(4,128)(2,1)S(1)}, u32[]{:S(2)}, u32[]{:S(2)}) collective-permute-start(bf16[4,768]{1,0:T(4,128)(2,1)S(1)} %get-tuple-element.34), channel_id=1, source_target_pairs={{0,8},{8,16},{16,24},{24,32},{32,40},{40,48},{48,56},{56,64},{64,7... | collective-permute-start | bytes 18440 | tf_op jit(solution)/shard_map/ppermute | solution.py:21
  5.7 9.4 %collective-permute-start.1 = (bf16[4,768]{1,0:T(4,128)(2,1)S(1)}, bf16[4,768]{1,0:T(4,128)(2,1)S(1)}, u32[]{:S(2)}, u32[]{:S(2)}) collective-permute-start(bf16[4,768]{1,0:T(4,128)(2,1)S(1)} %get-tuple-element.35), channel_id=1, source_target_pairs={{8,0},{16,8},{24,16},{32,24},{40,32},{48,40},{56,48},{64,56},{72,6... | collective-permute-start | bytes 18440 | tf_op jit(solution)/shard_map/ppermute | solution.py:23
  15.1 13.4 %copy-start.6 = (bf16[3,768,768]{2,1,0:T(8,128)(2,1)S(1)}, bf16[3,768,768]{2,1,0:T(8,128)(2,1)}, u32[]{:S(2)}) copy-start(bf16[3,768,768]{2,1,0:T(8,128)(2,1)} %param.12) | copy-start | bytes 10616836
  17.9 9.2 %collective-permute-start.2 = (bf16[16,768]{1,0:T(8,128)(2,1)S(1)}, bf16[16,768]{1,0:T(8,128)(2,1)S(1)}, u32[]{:S(2)}, u32[]{:S(2)}) collective-permute-start(bf16[16,768]{1,0:T(8,128)(2,1)S(1)} %get-tuple-element.32), channel_id=1, source_target_pairs={{0,8},{8,16},{16,24},{24,32},{32,40},{40,48},{48,56},{56,64},{64,7... | collective-permute-start | bytes 73736 | tf_op jit(solution)/shard_map/ppermute | solution.py:21
  19.8 8.8 %collective-permute-start.3 = (bf16[16,768]{1,0:T(8,128)(2,1)S(1)}, bf16[16,768]{1,0:T(8,128)(2,1)S(1)}, u32[]{:S(2)}, u32[]{:S(2)}) collective-permute-start(bf16[16,768]{1,0:T(8,128)(2,1)S(1)} %get-tuple-element.33), channel_id=1, source_target_pairs={{8,0},{16,8},{24,16},{32,24},{40,32},{48,40},{56,48},{64,56},{72,6... | collective-permute-start | bytes 73736 | tf_op jit(solution)/shard_map/ppermute | solution.py:23
  29.7 9.6 %collective-permute-start.4 = (bf16[64,768]{1,0:T(8,128)(2,1)S(1)}, bf16[64,768]{1,0:T(8,128)(2,1)S(1)}, u32[]{:S(2)}, u32[]{:S(2)}) collective-permute-start(bf16[64,768]{1,0:T(8,128)(2,1)S(1)} %get-tuple-element.30), channel_id=1, source_target_pairs={{0,8},{8,16},{16,24},{24,32},{32,40},{40,48},{48,56},{56,64},{64,7... | collective-permute-start | bytes 294920 | tf_op jit(solution)/shard_map/ppermute | solution.py:21
  31.6 9.5 %collective-permute-start.5 = (bf16[64,768]{1,0:T(8,128)(2,1)S(1)}, bf16[64,768]{1,0:T(8,128)(2,1)S(1)}, u32[]{:S(2)}, u32[]{:S(2)}) collective-permute-start(bf16[64,768]{1,0:T(8,128)(2,1)S(1)} %get-tuple-element.31), channel_id=1, source_target_pairs={{8,0},{16,8},{24,16},{32,24},{40,32},{48,40},{56,48},{64,56},{72,6... | collective-permute-start | bytes 294920 | tf_op jit(solution)/shard_map/ppermute | solution.py:23
  41.1 40.8 %copy-start.4 = (bf16[768,128]{1,0:T(8,128)(2,1)S(1)}, bf16[768,128]{1,0:T(8,128)(2,1)}, u32[]{:S(2)}) copy-start(bf16[768,128]{1,0:T(8,128)(2,1)} %param.13) | copy-start | bytes 589828
  41.1 40.9 %copy-start.3 = (bf16[768,128]{1,0:T(8,128)(2,1)S(1)}, bf16[768,128]{1,0:T(8,128)(2,1)}, u32[]{:S(2)}) copy-start(bf16[768,128]{1,0:T(8,128)(2,1)} %param.14) | copy-start | bytes 589828
  82.9 9.9 %collective-permute-start.6 = (bf16[1,512,128]{2,1,0:T(8,128)(2,1)S(1)}, bf16[1,512,128]{2,1,0:T(8,128)(2,1)S(1)}, u32[]{:S(2)}, u32[]{:S(2)}) collective-permute-start(bf16[1,512,128]{2,1,0:T(8,128)(2,1)S(1)} %get-tuple-element.28), channel_id=1, source_target_pairs={{0,8},{8,16},{16,24},{24,32},{32,40},{40,48},{48,56},{56,64},{64,7... | collective-permute-start | bytes 393224 | tf_op jit(solution)/shard_map/ppermute | solution.py:21
  85.2 9.4 %collective-permute-start.7 = (bf16[1,512,128]{2,1,0:T(8,128)(2,1)S(1)}, bf16[1,512,128]{2,1,0:T(8,128)(2,1)S(1)}, u32[]{:S(2)}, u32[]{:S(2)}) collective-permute-start(bf16[1,512,128]{2,1,0:T(8,128)(2,1)S(1)} %get-tuple-element.29), channel_id=1, source_target_pairs={{8,0},{16,8},{24,16},{32,24},{40,32},{48,40},{56,48},{64,56},{72,6... | collective-permute-start | bytes 393224 | tf_op jit(solution)/shard_map/ppermute | solution.py:23
  96.1 3.8 %copy-start.2 = (bf16[3,3,128,128]{3,2,1,0:T(8,128)(2,1)S(1)}, bf16[3,3,128,128]{3,2,1,0:T(8,128)(2,1)}, u32[]{:S(2)}) copy-start(bf16[3,3,128,128]{3,2,1,0:T(8,128)(2,1)} %param.15) | copy-start | bytes 884740
  105.8 3.3 %copy-start.1 = (bf16[512,768]{1,0:T(8,128)(2,1)S(1)}, bf16[512,768]{1,0:T(8,128)(2,1)}, u32[]{:S(2)}) copy-start(bf16[512,768]{1,0:T(8,128)(2,1)} %param.9) | copy-start | bytes 2359300
where the time goes:
time: 110 us; the launch traced here: 109 us
  blocking collectives  39 us (35%)
  starting transfers between devices  37.7 us (34%)
  matrix products  15.4 us (14%)
  waiting for transfers between devices  7.18 us (7%)
  local copies, waits for them, and re-layouts  6.22 us (6%)
  other arithmetic  2.74 us (2%)
    all_gather x1, blocking collectives, on_device(): lax.all_gather(pooled, 'seq', axis=0, tiled=True)  39 us
    ppermute x4, starting transfers between devices, with_halo(): lax.ppermute(head, axis, [((i + 1) % count, i) for i in range(ends)])  29.7 us
    dot_general x9, matrix products, pair_conv(): jnp.dot(window, pair_kernel[row_tap, col_tap], preferred_element_type=jnp...  8.85 us
    ppermute x4, starting transfers between devices, with_halo(): lax.ppermute(tail, axis, [(i, (i + 1) % count) for i in range(ends)])  8.02 us
    ppermute x4, waiting for transfers between devices, with_halo(): lax.ppermute(head, axis, [((i + 1) % count, i) for i in range(ends)])  6.28 us
    dot_general x3, matrix products, mix_rows(): jnp.dot(activated, point, preferred_element_type=jnp.float32)  5.33 us
    slice x1, local copies, waits for them, and re-layouts, pair_conv(): padded[row_tap:row_tap + rows, col_tap:col_tap + width]  3.77 us
  transfers between devices with their start and end apart: 8, of which 6 were waited for; matrix products, arithmetic and copies ran while one was open for 0% of the time, Pallas kernels for 0%

commit v1 on v0

v1 whole, which is shorter than its diff:
```python
import math

import jax
import jax.numpy as jnp
from jax import lax
from jax.experimental import pallas as pl
from jax.experimental.pallas import tpu as pltpu
from jax.sharding import Mesh
from jax.sharding import PartitionSpec as P

F32 = jnp.float32
BF16 = jnp.bfloat16
C = 768
PC = 128
BASES = 128
BINS = 8192
SLAB = 256
POOL = 16
HALO = 112
ROWS = SLAB + 2 * HALO
DILATIONS = (2, 8, 32)
STARTS = (16, 32, 96)
ENDS = (464, 448, 384)
STEP = 16

GELU_A = math.sqrt(2.0 / math.pi)
GELU_B = 0.044715 * GELU_A


def gelu_of_half(half):
    squared = half * half
    inner = half * (2.0 * GELU_A + (8.0 * GELU_B) * squared)
    return half + half * jnp.tanh(inner)


def trunk_kernel(
    own, low, high, table_hbm, gains, taps, point_hbm, query_w, key_w,
    trunk_out, keys_out, query_out,
    x_ref, n_ref, a_ref, table, point, sems,
):
    copies = [pltpu.make_async_copy(table_hbm, table, sems.at[0])]
    for layer in range(3):
        copies.append(
            pltpu.make_async_copy(point_hbm.at[layer], point.at[layer], sems.at[1 + layer])
        )
    for copy in copies:
        copy.start()
    place = lax.axis_index(("x_hi", "z", "core"))
    first_bin = place * SLAB - HALO

    spread = (
        lax.broadcasted_iota(jnp.int32, (BASES, 4 * BASES), 1) // 4
        == lax.broadcasted_iota(jnp.int32, (BASES, 4 * BASES), 0)
    ).astype(F32).astype(BF16)
    copies[0].wait()

    def embed(codes, at, count):
        repeated = jnp.dot(codes.astype(F32).astype(BF16), spread, preferred_element_type=F32)
        base = (lax.broadcasted_iota(jnp.int32, (count, 4 * BASES), 1) % 4).astype(F32)
        one_hot = jnp.where(repeated == base, 1.0, 0.0).astype(BF16)
        x_ref[at : at + count, :] = jnp.dot(one_hot, table[...], preferred_element_type=F32)

    embed(low[...], 0, HALO)
    embed(own[0:128, :], HALO, 128)
    embed(own[128:256, :], HALO + 128, 128)
    embed(high[...], HALO + SLAB, HALO)

    for layer in range(3):
        reach = DILATIONS[layer]
        in_start = STARTS[layer] - max(8, 2 * reach)
        in_end = ENDS[layer] + max(8, 2 * reach)
        gain = gains[layer : layer + 1, :]

        def norm_step(j, _, in_start=in_start, gain=gain):
            at = pl.multiple_of(in_start + j * STEP, 8)
            rows = x_ref[pl.ds(at, STEP), :]
            mean = jnp.sum(rows * rows, axis=-1, keepdims=True) * (1.0 / C)
            bins = first_bin + at + lax.broadcasted_iota(jnp.int32, (STEP, 1), 0)
            inside = (bins >= 0) & (bins < BINS)
            scale = jnp.where(inside, lax.rsqrt(mean + 1e-06), 0.0)
            n_ref[pl.ds(at, STEP), :] = rows * scale * gain
            return 0

        lax.fori_loop(0, (in_end - in_start) // STEP, norm_step, 0, unroll=2)

        tap_rows = [taps[layer, t : t + 1, :] * 0.5 for t in range(5)]
        start = STARTS[layer]

        def conv_step(j, _, start=start, reach=reach, tap_rows=tap_rows):
            at = pl.multiple_of(start + j * STEP, 8)
            if reach % 8:
                wide = n_ref[pl.ds(pl.multiple_of(at - 8, 8), STEP + 16), :]
                pieces = [wide[8 + (t - 2) * reach : 8 + (t - 2) * reach + STEP] for t in range(5)]
            else:
                pieces = [
                    n_ref[pl.ds(pl.multiple_of(at + (t - 2) * reach, 8), STEP), :] for t in range(5)
                ]
            half = pieces[0] * tap_rows[0]
            for t in range(1, 5):
                half = half + pieces[t] * tap_rows[t]
            a_ref[pl.ds(pl.multiple_of(at, 16), STEP), :] = gelu_of_half(half).astype(BF16)
            return 0

        lax.fori_loop(0, (ENDS[layer] - start) // STEP, conv_step, 0, unroll=2)
        copies[1 + layer].wait()
        for strip in range(3):
            cols = slice(strip * 256, strip * 256 + 256)
            update = jnp.dot(
                a_ref[start : ENDS[layer], :], point[layer, :, cols], preferred_element_type=F32
            )
            total = x_ref[start : ENDS[layer], cols] + update
            if layer < 2:
                x_ref[start : ENDS[layer], cols] = total
            else:
                n_ref[start : ENDS[layer], cols] = total

    trunk = n_ref[STARTS[2] : ENDS[2], :].astype(BF16)
    trunk_out[...] = trunk[POOL : POOL + SLAB, :]
    count = ENDS[2] - STARTS[2]
    pooling = jnp.where(
        lax.broadcasted_iota(jnp.int32, (32, count), 1) // POOL
        == lax.broadcasted_iota(jnp.int32, (32, count), 0),
        1.0 / POOL,
        0.0,
    ).astype(BF16)
    pooled = jnp.dot(pooling, trunk, preferred_element_type=F32).astype(BF16)
    queries = jnp.dot(pooled, query_w[...], preferred_element_type=F32).astype(BF16).astype(F32)
    keys = jnp.dot(pooled, key_w[...], preferred_element_type=F32)
    row = place * (SLAB // POOL) - 1 + lax.broadcasted_iota(jnp.int32, (32, PC), 0)
    query_out[...] = jnp.where((row >= 0) & (row < BINS // POOL), queries, 0.0)
    mine = pltpu.roll(keys, 31, 0)[0:16].astype(BF16)
    for peer in range(16):
        keys_out[peer] = mine


def pair_kernel_body(
    queries, own, other, kernel, out_hbm, wide_q, kernel_f, key_f, key_cat, out_ref, weights, sems
):
    core = lax.axis_index("core")
    flipped = jnp.transpose(queries[...], (1, 0))
    for i in range(18):
        wide_q[i] = jnp.broadcast_to(flipped[:, i : i + 1] * 0.5, (PC, PC))
    for t in range(9):
        kernel_f[t] = kernel[t // 3, t % 3].astype(F32)
    for g in range(16):
        mine = own[g]
        theirs = other[g]
        key_cat[g * 32 : g * 32 + 16, PC : 2 * PC] = jnp.where(core == 0, mine, theirs)
        key_cat[g * 32 + 16 : g * 32 + 32, PC : 2 * PC] = jnp.where(core == 0, theirs, mine)
    keys = key_cat[:, PC : 2 * PC].astype(F32)
    key_f[...] = keys
    at = lax.broadcasted_iota(jnp.int32, keys.shape, 0)
    before = jnp.where(at == 0, 0.0, pltpu.roll(keys, 1, 0))
    after = jnp.where(at == 511, 0.0, pltpu.roll(keys, 511, 0))
    key_cat[:, 0:PC] = before.astype(BF16)
    key_cat[:, 2 * PC : 3 * PC] = after.astype(BF16)

    def copy_of(i):
        return pltpu.make_async_copy(
            out_ref.at[pl.ds(2 * i, 2)], out_hbm.at[pl.ds(2 * i, 2)], sems.at[i]
        )

    def two_rows(i, _):
        for r in range(2):
            row = 2 * i + r
            for b in range(3):
                mixed = wide_q[row] * kernel_f[b]
                mixed = mixed + wide_q[row + 1] * kernel_f[3 + b]
                mixed = mixed + wide_q[row + 2] * kernel_f[6 + b]
                weights[b * PC : (b + 1) * PC, r * PC : (r + 1) * PC] = mixed.astype(BF16)
        for m in range(4):
            rows = slice(m * 128, m * 128 + 128)
            half = jnp.dot(key_cat[rows, :], weights[...], preferred_element_type=F32)
            for r in range(2):
                query = queries[pl.ds(2 * i + r + 1, 1), :]
                pair = key_f[rows, :] * query
                value = pair + gelu_of_half(half[:, r * PC : (r + 1) * PC])
                out_ref[2 * i + r, rows, :] = value.astype(BF16)
        copy_of(i).start()
        return 0

    lax.fori_loop(0, 8, two_rows, 0)

    def finish(i, _):
        copy_of(i).wait()
        return 0

    lax.fori_loop(0, 8, finish, 0)


def vmem(count):
    return [pl.BlockSpec(memory_space=pltpu.VMEM)] * count


def on_device(
    bases, embed_table, norm_gains, depth_taps, point_weight, query_weight, key_weight, pair_kernel
):
    core = lax.axis_index("core")
    seq = ("x_hi", "z", "core")
    head_first = jnp.where(core == 0, SLAB - HALO, 0)
    inner_send = lax.dynamic_slice(bases, (head_first, 0), (HALO, BASES))
    outer_send = lax.dynamic_slice(bases, (SLAB - HALO - head_first, 0), (HALO, BASES))
    outer_pairs = []
    for i in range(1, 31, 2):
        outer_pairs += [(i, i + 1), (i + 1, i)]
    outer = lax.ppermute(outer_send, seq, outer_pairs)
    inner = lax.ppermute(inner_send, "core", [(0, 1), (1, 0)])
    low = jnp.where(core == 0, outer, inner)
    high = jnp.where(core == 0, inner, outer)

    any_space = [pl.BlockSpec(memory_space=pl.ANY)]
    trunk, keys, queries = pl.pallas_call(
        trunk_kernel,
        out_shape=(
            jax.ShapeDtypeStruct((SLAB, C), BF16),
            jax.ShapeDtypeStruct((16, 16, PC), BF16),
            jax.ShapeDtypeStruct((32, PC), F32),
        ),
        in_specs=vmem(3) + any_space + vmem(2) + any_space + vmem(2),
        out_specs=tuple(vmem(3)),
        scratch_shapes=[
            pltpu.VMEM((ROWS, C), F32),
            pltpu.VMEM((ROWS, C), F32),
            pltpu.VMEM((ROWS, C), BF16),
            pltpu.VMEM((4 * BASES, C), BF16),
            pltpu.VMEM((3, C, C), BF16),
            pltpu.SemaphoreType.DMA((4,)),
        ],
        compiler_params=pltpu.CompilerParams(vmem_limit_bytes=40 * 1024 * 1024),
        name="trunk",
    )(bases, low, high, embed_table, norm_gains, depth_taps, point_weight, query_weight, key_weight)

    own_keys = lax.all_to_all(keys, ("x_hi", "z"), 0, 0, tiled=False)
    other_keys = lax.ppermute(own_keys, "core", [(0, 1), (1, 0)])

    pair_map = pl.pallas_call(
        pair_kernel_body,
        out_shape=jax.ShapeDtypeStruct((16, 512, PC), BF16),
        in_specs=vmem(4),
        out_specs=pl.BlockSpec(memory_space=pl.ANY),
        scratch_shapes=[
            pltpu.VMEM((18, PC, PC), F32),
            pltpu.VMEM((9, PC, PC), F32),
            pltpu.VMEM((512, PC), F32),
            pltpu.VMEM((512, 3 * PC), BF16),
            pltpu.VMEM((16, 512, PC), BF16),
            pltpu.VMEM((3 * PC, 2 * PC), BF16),
            pltpu.SemaphoreType.DMA((8,)),
        ],
        compiler_params=pltpu.CompilerParams(vmem_limit_bytes=24 * 1024 * 1024),
        name="pair",
    )(queries, own_keys, other_keys, pair_kernel)
    return (trunk, pair_map)


def solution(mesh):
    devices = mesh.devices.reshape(2, 8, 2, -1)
    fine = Mesh(devices, ("x_hi", "z", "core", "batch"))
    rows = ("batch", "x_hi", "z", "core")
    return jax.shard_map(
        on_device,
        mesh=fine,
        in_specs=(P(rows, None), P(), P(), P(), P(), P(), P(), P()),
        out_specs=(P(rows, None), P(rows, None, None)),
        check_vma=False,
    )
```

time: 110 us -> 56.2 us (0.51)
  the two profiles are of different devices: /device:TPU:14 before, /device:TPU:1 now
where the time goes in v1:
time: 56.2 us; the launch traced here: 55.8 us
  blocking collectives  18.1 us (32%)
  Pallas kernels  17.6 us (31%)
  local copies, waits for them, and re-layouts  8.34 us (15%)
  starting transfers between devices  7.47 us (13%)
  waiting for transfers between devices  3.61 us (6%)
  between operations  0.7 us (1%)
    all_to_all x1, blocking collectives, on_device(): own_keys = lax.all_to_all(keys, ('x_hi', 'z'), 0, 0, tiled=False)  18.1 us
    pallas_call x1, Pallas kernels, on_device(): pl.pallas_call(trunk_kernel, out_shape=(jax.ShapeDtypeStruct((SLAB, C), B...  12.8 us
    unnamed x15, local copies, waits for them, and re-layouts  7.44 us
    pallas_call x1, Pallas kernels, on_device(): pl.pallas_call(pair_kernel_body, out_shape=jax.ShapeDtypeStruct((16, 512,...  4.82 us
    ppermute x1, starting transfers between devices, on_device(): inner = lax.ppermute(inner_send, 'core', [(0, 1), (1, 0)])  3.28 us
    ppermute x1, waiting for transfers between devices, on_device(): outer = lax.ppermute(outer_send, seq, outer_pairs)  2.71 us
    ppermute x1, starting transfers between devices, on_device(): other_keys = lax.ppermute(own_keys, 'core', [(0, 1), (1, 0)])  2.28 us
    ppermute x1, starting transfers between devices, on_device(): outer = lax.ppermute(outer_send, seq, outer_pairs)  1.91 us
  transfers between devices with their start and end apart: 3, of which 2 were waited for; matrix products, arithmetic and copies ran while one was open for 2% of the time, Pallas kernels for 0%

profile of v1, /device:TPU:1, one launch (start us, length us, event | category | flops | bytes accessed | tf_op | source)
XLA Modules:
  0.0 55.8 jit_solution(13275452085772029882)
XLA Ops:
  0.6 0.0 copy-start.3
  0.6 0.9 %constant_dynamic-slice_fusion = (s32[112,128]{1,0:T(8,128)S(1)}, s32[112,128]{1,0:T(8,128)S(1)}) fusion(s32[256,128]{1,0:T(8,128)} %own.1, s32[]{:T(128)S(6)} %select_n.21, s32[]{:T(128)S(6)} %select_n.22), kind=kLoop, calls=%fused_computation.2 | loop fusion | bytes 229384 | tf_op jit(solution)/shard_map/dynamic_slice | solution.py:201
  1.6 3.3 %collective-permute-start.1 = (s32[112,128]{1,0:T(8,128)S(1)}, s32[112,128]{1,0:T(8,128)S(1)}, u32[]{:S(2)}, u32[]{:S(2)}) collective-permute-start(s32[112,128]{1,0:T(8,128)S(1)} %get-tuple-element.8), channel_id=1, source_target_pairs={{0,8},{8,0},{1,9},{9,1},{2,10},{10,2},{3,11},{11,3},{4,12},{12,4},... | collective-permute-start | bytes 172040 | tf_op jit(solution)/shard_map/ppermute | solution.py:207
  4.8 1.9 %collective-permute-start = (s32[112,128]{1,0:T(8,128)S(1)}, s32[112,128]{1,0:T(8,128)S(1)}, u32[]{:S(2)}, u32[]{:S(2)}) collective-permute-start(s32[112,128]{1,0:T(8,128)S(1)} %get-tuple-element.9), channel_id=1, source_target_pairs={{8,16},{16,8},{24,32},{32,24},{40,48},{48,40},{56,64},{64,56},{72,... | collective-permute-start | bytes 172040 | tf_op jit(solution)/shard_map/ppermute | solution.py:206
  6.8 0.8 %copy.10.taps = f32[3,5,768]{2,1,0:T(8,128)S(1)} copy(f32[3,5,768]{2,0,1:T(4,128)} %param.11) | data formatting | bytes 92160 | tf_op args[3]
  7.6 0.0 collective-permute-done.1
  7.6 2.7 %collective-permute-done = s32[112,128]{1,0:T(8,128)S(1)} collective-permute-done((s32[112,128]{1,0:T(8,128)S(1)}, s32[112,128]{1,0:T(8,128)S(1)}, u32[]{:S(2)}, u32[]{:S(2)}) %collective-permute-start) | collective-permute-done | bytes 57376 | tf_op jit(solution)/shard_map/ppermute | solution.py:206
  10.3 0.0 copy-start
  10.3 2.0 %copy-done = bf16[3,768,768]{2,1,0:T(8,128)(2,1)S(1)} copy-done((bf16[3,768,768]{2,1,0:T(8,128)(2,1)S(1)}, bf16[3,768,768]{2,1,0:T(8,128)(2,1)}, u32[]{:S(2)}) %copy-start) | copy-done | bytes 3538968
  12.3 0.0 copy-start.1
  12.3 1.1 %copy-done.1 = bf16[512,768]{1,0:T(8,128)(2,1)S(1)} copy-done((bf16[512,768]{1,0:T(8,128)(2,1)S(1)}, bf16[512,768]{1,0:T(8,128)(2,1)}, u32[]{:S(2)}) %copy-start.1) | copy-done | bytes 786456
  13.5 0.0 copy-start.2
  13.5 0.9 %copy-done.2 = s32[256,128]{1,0:T(8,128)S(1)} copy-done((s32[256,128]{1,0:T(8,128)S(1)}, s32[256,128]{1,0:T(8,128)}, u32[]{:S(2)}) %copy-start.2) | copy-done | bytes 131096
  14.4 0.0 copy-start.4
  14.4 0.9 %copy-done.4 = bf16[768,128]{1,0:T(8,128)(2,1)S(1)} copy-done((bf16[768,128]{1,0:T(8,128)(2,1)S(1)}, bf16[768,128]{1,0:T(8,128)(2,1)}, u32[]{:S(2)}) %copy-start.4) | copy-done | bytes 196632
  15.3 0.0 copy-start.5
  15.3 0.9 %copy-done.5 = bf16[768,128]{1,0:T(8,128)(2,1)S(1)} copy-done((bf16[768,128]{1,0:T(8,128)(2,1)S(1)}, bf16[768,128]{1,0:T(8,128)(2,1)}, u32[]{:S(2)}) %copy-start.5) | copy-done | bytes 196632
  16.2 0.0 copy-start.6
  16.2 0.7 %copy-done.6 = f32[3,768]{1,0:T(4,128)S(1)} copy-done((f32[3,768]{1,0:T(4,128)S(1)}, f32[3,768]{1,0:T(4,128)}, u32[]{:S(2)}) %copy-start.6) | copy-done | bytes 9240
  16.9 12.8 %trunk.1 = (bf16[256,768]{1,0:T(8,128)(2,1)}, bf16[16,16,128]{2,1,0:T(8,128)(2,1)S(1)}, f32[32,128]{1,0:T(8,128)S(1)}) custom-call(s32[256,128]{1,0:T(8,128)S(1)} %copy-done.2, s32[112,128]{1,0:T(8,128)S(1)} %get-tuple-element.11.low, s32[112,128]{1,0:T(8,128)S(1)} %get-tuple-element.10.high, bf16[512,768]{1,0:T(8,128)(2,1)S(1)} %copy-done.1, ...), custom_call_target="tpu_custom_call" | custom-call | tf_op jit(solution)/shard_map/trunk/pallas_call | solution.py:212
  29.7 18.1 %all_to_all.5.own = bf16[16,16,128]{2,1,0:T(8,128)(2,1)S(1)} all-to-all(bf16[16,16,128]{2,1,0:T(8,128)(2,1)S(1)} %get-tuple-element.7), channel_id=1, replica_groups=mesh['x_hi'=2,'z'=8,'core'=2,'batch'=8] {'x_hi','z'}, dimensions={0} | all-to-all | bytes 131072 | tf_op jit(solution)/shard_map/all_to_all | solution.py:233
  47.8 2.3 %collective-permute-start.2 = (bf16[16,16,128]{2,1,0:T(8,128)(2,1)S(1)}, bf16[16,16,128]{2,1,0:T(8,128)(2,1)S(1)}, u32[]{:S(2)}, u32[]{:S(2)}) collective-permute-start(bf16[16,16,128]{2,1,0:T(8,128)(2,1)S(1)} %all_to_all.5.own), channel_id=1, source_target_pairs={{0,8},{8,0},{1,9},{9,1},{2,10},{10,2},{3,11},{11,3},{4,12},{12,4},... | collective-permute-start | bytes 196616 | tf_op jit(solution)/shard_map/ppermute | solution.py:234
  50.1 0.9 %collective-permute-done.2.other = bf16[16,16,128]{2,1,0:T(8,128)(2,1)S(1)} collective-permute-done((bf16[16,16,128]{2,1,0:T(8,128)(2,1)S(1)}, bf16[16,16,128]{2,1,0:T(8,128)(2,1)S(1)}, u32[]{:S(2)}, u32[]{:S(2)}) %collective-permute-start.2) | collective-permute-done | bytes 65568 | tf_op jit(solution)/shard_map/ppermute | solution.py:234
  51.0 0.0 copy-done.3
  51.0 4.8 %pair.1 = bf16[16,512,128]{2,1,0:T(8,128)(2,1)} custom-call(f32[32,128]{1,0:T(8,128)S(1)} %get-tuple-element.6.queries, bf16[16,16,128]{2,1,0:T(8,128)(2,1)S(1)} %all_to_all.5.own, bf16[16,16,128]{2,1,0:T(8,128)(2,1)S(1)} %collective-permute-done.2.other, bf16[3,3,128,128]{3,2,1,0:T(8,128)(2,1)S(1)} %copy-done.3), custom_call_target="tpu_custom_call" | custom-call | tf_op jit(solution)/shard_map/pair/pallas_call | solution.py:236
  (1 shorter events, 0.0 us)
Async XLA Ops:
  0.6 50.4 %copy-start.3 = (bf16[3,3,128,128]{3,2,1,0:T(8,128)(2,1)S(1)}, bf16[3,3,128,128]{3,2,1,0:T(8,128)(2,1)}, u32[]{:S(2)}) copy-start(bf16[3,3,128,128]{3,2,1,0:T(8,128)(2,1)} %kernel.1) | copy-start | bytes 884740
  1.6 6.1 %collective-permute-start.1 = (s32[112,128]{1,0:T(8,128)S(1)}, s32[112,128]{1,0:T(8,128)S(1)}, u32[]{:S(2)}, u32[]{:S(2)}) collective-permute-start(s32[112,128]{1,0:T(8,128)S(1)} %get-tuple-element.8), channel_id=1, source_target_pairs={{0,8},{8,0},{1,9},{9,1},{2,10},{10,2},{3,11},{11,3},{4,12},{12,4},... | collective-permute-start | bytes 172040 | tf_op jit(solution)/shard_map/ppermute | solution.py:207
  4.8 5.5 %collective-permute-start = (s32[112,128]{1,0:T(8,128)S(1)}, s32[112,128]{1,0:T(8,128)S(1)}, u32[]{:S(2)}, u32[]{:S(2)}) collective-permute-start(s32[112,128]{1,0:T(8,128)S(1)} %get-tuple-element.9), channel_id=1, source_target_pairs={{8,16},{16,8},{24,32},{32,24},{40,48},{48,40},{56,64},{64,56},{72,... | collective-permute-start | bytes 172040 | tf_op jit(solution)/shard_map/ppermute | solution.py:206
  10.3 2.0 %copy-start = (bf16[3,768,768]{2,1,0:T(8,128)(2,1)S(1)}, bf16[3,768,768]{2,1,0:T(8,128)(2,1)}, u32[]{:S(2)}) copy-start(bf16[3,768,768]{2,1,0:T(8,128)(2,1)} %point_hbm.1) | copy-start | bytes 10616836
  12.3 1.1 %copy-start.1 = (bf16[512,768]{1,0:T(8,128)(2,1)S(1)}, bf16[512,768]{1,0:T(8,128)(2,1)}, u32[]{:S(2)}) copy-start(bf16[512,768]{1,0:T(8,128)(2,1)} %table_hbm.1) | copy-start | bytes 2359300
  13.5 0.9 %copy-start.2 = (s32[256,128]{1,0:T(8,128)S(1)}, s32[256,128]{1,0:T(8,128)}, u32[]{:S(2)}) copy-start(s32[256,128]{1,0:T(8,128)} %own.1) | copy-start | bytes 393220
  14.4 0.9 %copy-start.4 = (bf16[768,128]{1,0:T(8,128)(2,1)S(1)}, bf16[768,128]{1,0:T(8,128)(2,1)}, u32[]{:S(2)}) copy-start(bf16[768,128]{1,0:T(8,128)(2,1)} %query_w.1) | copy-start | bytes 589828
  15.3 0.9 %copy-start.5 = (bf16[768,128]{1,0:T(8,128)(2,1)S(1)}, bf16[768,128]{1,0:T(8,128)(2,1)}, u32[]{:S(2)}) copy-start(bf16[768,128]{1,0:T(8,128)(2,1)} %key_w.1) | copy-start | bytes 589828
  16.2 0.7 %copy-start.6 = (f32[3,768]{1,0:T(4,128)S(1)}, f32[3,768]{1,0:T(4,128)}, u32[]{:S(2)}) copy-start(f32[3,768]{1,0:T(4,128)} %gains.1) | copy-start | bytes 27652
  47.8 3.2 %collective-permute-start.2 = (bf16[16,16,128]{2,1,0:T(8,128)(2,1)S(1)}, bf16[16,16,128]{2,1,0:T(8,128)(2,1)S(1)}, u32[]{:S(2)}, u32[]{:S(2)}) collective-permute-start(bf16[16,16,128]{2,1,0:T(8,128)(2,1)S(1)} %all_to_all.5.own), channel_id=1, source_target_pairs={{0,8},{8,0},{1,9},{9,1},{2,10},{10,2},{3,11},{11,3},{4,12},{12,4},... | collective-permute-start | bytes 196616 | tf_op jit(solution)/shard_map/ppermute | solution.py:234

commit v2 on v1

v2 whole, which is shorter than its diff:
```python
import math

import jax
import jax.numpy as jnp
from jax import lax
from jax.experimental import pallas as pl
from jax.experimental.pallas import tpu as pltpu
from jax.sharding import Mesh
from jax.sharding import PartitionSpec as P

F32 = jnp.float32
BF16 = jnp.bfloat16
C = 768
PC = 128
BASES = 128
BINS = 8192
SLAB = 256
POOL = 16
HALO = 112
ROWS = SLAB + 2 * HALO
DILATIONS = (2, 8, 32)
STEP = 16

GELU_A = math.sqrt(2.0 / math.pi)
GELU_B = 0.044715 * GELU_A


def gelu_of_half(half):
    squared = half * half
    inner = half * (2.0 * GELU_A + (8.0 * GELU_B) * squared)
    return half + half * jnp.tanh(inner)


def spread_matrix():
    return (
        lax.broadcasted_iota(jnp.int32, (BASES, 4 * BASES), 1) // 4
        == lax.broadcasted_iota(jnp.int32, (BASES, 4 * BASES), 0)
    ).astype(F32).astype(BF16)


def embed(codes, spread, table):
    repeated = jnp.dot(codes.astype(F32).astype(BF16), spread, preferred_element_type=F32)
    base = (lax.broadcasted_iota(jnp.int32, repeated.shape, 1) % 4).astype(F32)
    one_hot = jnp.where(repeated == base, 1.0, 0.0).astype(BF16)
    return jnp.dot(one_hot, table[...], preferred_element_type=F32)


def norm_rows(x_ref, n_ref, layer, count, row_of, scale_of, unroll):
    def step(j, _):
        at = pl.multiple_of(row_of(j), STEP)
        rows = x_ref[pl.ds(at, STEP), :]
        mean = jnp.sum(rows * rows, axis=-1, keepdims=True) * (1.0 / C)
        rows = rows * (lax.rsqrt(mean + 1e-06) * scale_of(at))
        for c in range(C // 128):
            n_ref[layer, c, pl.ds(at, STEP), :] = rows[:, c * 128 : (c + 1) * 128]
        return 0

    lax.fori_loop(0, count, step, 0, unroll=unroll)


def conv_rows(n_ref, a_ref, layer, gains, taps, count, row_of, unroll):
    reach = DILATIONS[layer]
    gain = gains[layer : layer + 1, :] * 0.5
    tap_rows = [taps[t, layer : layer + 1, :] * gain for t in range(5)]

    def step(j, _):
        at = row_of(j)
        to = pl.multiple_of(j * STEP, STEP)
        for c in range(C // 128):
            cols = slice(c * 128, (c + 1) * 128)
            half = None
            for t in range(5):
                piece = n_ref[layer, c, pl.ds(at + (t - 2) * reach, STEP), :]
                term = piece * tap_rows[t][:, cols]
                half = term if half is None else half + term
            a_ref[pl.ds(to, STEP), cols] = gelu_of_half(half).astype(BF16)
        return 0

    lax.fori_loop(0, count, step, 0, unroll=unroll)


def mix(a_ref, x_ref, weights, spans):
    total = sum(stop - start for start, stop in spans)
    for strip in range(3):
        cols = slice(strip * 256, strip * 256 + 256)
        update = jnp.dot(a_ref[0:total, :], weights[:, cols], preferred_element_type=F32)
        done = 0
        for start, stop in spans:
            x_ref[start:stop, cols] = x_ref[start:stop, cols] + update[done : done + stop - start]
            done += stop - start


def inner_kernel(own, table_hbm, gains, taps, point_hbm, x_ref, n_ref, table, point, a_ref, sems):
    copies = [pltpu.make_async_copy(table_hbm, table, sems.at[0])]
    for layer in range(3):
        copies.append(
            pltpu.make_async_copy(point_hbm.at[layer], point.at[layer], sems.at[1 + layer])
        )
    for copy in copies:
        copy.start()
    spread = spread_matrix()
    copies[0].wait()
    for half in range(2):
        at = HALO + half * 128
        x_ref[at : at + 128, :] = embed(own[half * 128 : half * 128 + 128, :], spread, table)

    def one(at):
        return 1.0

    norm_rows(x_ref, n_ref, 0, 16, lambda j: HALO + j * STEP, one, 4)
    conv_rows(n_ref, a_ref, 0, gains, taps, 14, lambda j: 128 + j * STEP, 2)
    copies[1].wait()
    mix(a_ref, x_ref, point.at[0], ((128, 352),))
    norm_rows(x_ref, n_ref, 1, 14, lambda j: 128 + j * STEP, one, 7)
    conv_rows(n_ref, a_ref, 1, gains, taps, 12, lambda j: 144 + j * STEP, 2)
    copies[2].wait()
    mix(a_ref, x_ref, point.at[1], ((144, 336),))
    norm_rows(x_ref, n_ref, 2, 12, lambda j: 144 + j * STEP, one, 4)
    copies[3].wait()


def outer_kernel(
    inner, outer, gains, taps, table, point, query_w, key_w, x_in, n_in,
    trunk_out, keys_out, query_out, x_ref, n_ref, a_ref,
):
    del x_in, n_in
    place = lax.axis_index(("x_hi", "z", "core"))
    core = lax.axis_index("core")
    low_bases = jnp.where(core == 0, outer[SLAB - HALO :, :], inner[SLAB - HALO :, :])
    high_bases = jnp.where(core == 0, inner[:HALO, :], outer[:HALO, :])
    spread = spread_matrix()
    both = embed(jnp.concatenate([low_bases, high_bases], axis=0), spread, table)
    x_ref[0:HALO, :] = both[0:HALO]
    x_ref[HALO + SLAB :, :] = both[HALO:]

    def inside(at):
        gone = ((at < HALO) & (place == 0)) | ((at >= HALO + SLAB) & (place == 31))
        return jnp.where(gone, 0.0, 1.0)

    def two_spans(low, high):
        return lambda j: jnp.where(j < 7, low + j * STEP, high + (j - 7) * STEP)

    norm_rows(x_ref, n_ref, 0, 14, two_spans(0, 368), inside, 7)
    conv_rows(n_ref, a_ref, 0, gains, taps, 14, two_spans(16, 352), 2)
    mix(a_ref, x_ref, point.at[0], ((16, 128), (352, 464)))
    norm_rows(x_ref, n_ref, 1, 14, two_spans(16, 352), inside, 7)
    conv_rows(n_ref, a_ref, 1, gains, taps, 14, two_spans(32, 336), 2)
    mix(a_ref, x_ref, point.at[1], ((32, 144), (336, 448)))
    norm_rows(x_ref, n_ref, 2, 14, two_spans(32, 336), inside, 7)
    conv_rows(n_ref, a_ref, 2, gains, taps, 18, lambda j: 96 + j * STEP, 2)
    mix(a_ref, x_ref, point.at[2], ((96, 384),))

    trunk = x_ref[96:384, :].astype(BF16)
    trunk_out[...] = trunk[POOL : POOL + SLAB, :]
    pooling = jnp.where(
        lax.broadcasted_iota(jnp.int32, (32, 288), 1) // POOL
        == lax.broadcasted_iota(jnp.int32, (32, 288), 0),
        1.0 / POOL,
        0.0,
    ).astype(BF16)
    pooled = jnp.dot(pooling, trunk, preferred_element_type=F32).astype(BF16)
    queries = jnp.dot(pooled, query_w[...], preferred_element_type=F32).astype(BF16).astype(F32)
    keys = jnp.dot(pooled, key_w[...], preferred_element_type=F32)
    row = place * (SLAB // POOL) - 1 + lax.broadcasted_iota(jnp.int32, (32, PC), 0)
    query_out[...] = jnp.where((row >= 0) & (row < BINS // POOL), queries, 0.0)
    mine = pltpu.roll(keys, 31, 0)[0:16].astype(BF16)
    for peer in range(16):
        keys_out[peer] = mine


def pair_kernel_body(
    queries, own, other, kernel, out_hbm, wide_q, kernel_f, key_f, key_cat, out_ref, weights, sems
):
    core = lax.axis_index("core")
    flipped = jnp.transpose(queries[...], (1, 0))
    for i in range(18):
        wide_q[i] = jnp.broadcast_to(flipped[:, i : i + 1] * 0.5, (PC, PC))
    for t in range(9):
        kernel_f[t] = kernel[t // 3, t % 3].astype(F32)
    for g in range(16):
        mine = own[g]
        theirs = other[g]
        key_cat[g * 32 : g * 32 + 16, PC : 2 * PC] = jnp.where(core == 0, mine, theirs)
        key_cat[g * 32 + 16 : g * 32 + 32, PC : 2 * PC] = jnp.where(core == 0, theirs, mine)
    keys = key_cat[:, PC : 2 * PC].astype(F32)
    key_f[...] = keys
    at = lax.broadcasted_iota(jnp.int32, keys.shape, 0)
    before = jnp.where(at == 0, 0.0, pltpu.roll(keys, 1, 0))
    after = jnp.where(at == 511, 0.0, pltpu.roll(keys, 511, 0))
    key_cat[:, 0:PC] = before.astype(BF16)
    key_cat[:, 2 * PC : 3 * PC] = after.astype(BF16)

    def copy_of(i):
        return pltpu.make_async_copy(
            out_ref.at[pl.ds(2 * i, 2)], out_hbm.at[pl.ds(2 * i, 2)], sems.at[i]
        )

    def two_rows(i, _):
        for r in range(2):
            row = 2 * i + r
            for b in range(3):
                mixed = wide_q[row] * kernel_f[b]
                mixed = mixed + wide_q[row + 1] * kernel_f[3 + b]
                mixed = mixed + wide_q[row + 2] * kernel_f[6 + b]
                weights[b * PC : (b + 1) * PC, r * PC : (r + 1) * PC] = mixed.astype(BF16)
        for m in range(4):
            rows = slice(m * 128, m * 128 + 128)
            half = jnp.dot(key_cat[rows, :], weights[...], preferred_element_type=F32)
            for r in range(2):
                query = queries[pl.ds(2 * i + r + 1, 1), :]
                pair = key_f[rows, :] * query
                value = pair + gelu_of_half(half[:, r * PC : (r + 1) * PC])
                out_ref[2 * i + r, rows, :] = value.astype(BF16)
        copy_of(i).start()
        return 0

    lax.fori_loop(0, 8, two_rows, 0)

    def finish(i, _):
        copy_of(i).wait()
        return 0

    lax.fori_loop(0, 8, finish, 0)


def in_hbm(array):
    return pltpu.with_memory_space_constraint(array, pltpu.HBM)


def vmem(count):
    return [pl.BlockSpec(memory_space=pltpu.VMEM)] * count


def on_device(
    bases, embed_table, norm_gains, depth_taps, point_weight, query_weight, key_weight, pair_kernel
):
    seq = ("x_hi", "z", "core")
    outer_pairs = []
    for i in range(1, 31, 2):
        outer_pairs += [(i, i + 1), (i + 1, i)]
    inner = lax.ppermute(bases, "core", [(0, 1), (1, 0)])
    outer = lax.ppermute(bases, seq, outer_pairs)

    taps = jnp.transpose(depth_taps, (1, 0, 2))
    hbm_space = [pl.BlockSpec(memory_space=pltpu.HBM)]
    state = (
        jax.ShapeDtypeStruct((ROWS, C), F32),
        jax.ShapeDtypeStruct((3, C // 128, ROWS, 128), F32),
    )
    x, n, table, point = pl.pallas_call(
        inner_kernel,
        out_shape=state
        + (
            jax.ShapeDtypeStruct((4 * BASES, C), BF16),
            jax.ShapeDtypeStruct((3, C, C), BF16),
        ),
        in_specs=vmem(1) + hbm_space + vmem(2) + hbm_space,
        out_specs=tuple(vmem(4)),
        scratch_shapes=[pltpu.VMEM((SLAB, C), BF16), pltpu.SemaphoreType.DMA((4,))],
        compiler_params=pltpu.CompilerParams(vmem_limit_bytes=16 * 1024 * 1024),
        cost_estimate=pl.CostEstimate(
            flops=800_000_000, bytes_accessed=5_000_000, transcendentals=400_000
        ),
        name="inner",
    )(in_hbm(bases), in_hbm(embed_table), in_hbm(norm_gains), in_hbm(taps), in_hbm(point_weight))
    trunk, keys, queries, _, _ = pl.pallas_call(
        outer_kernel,
        out_shape=(
            jax.ShapeDtypeStruct((SLAB, C), BF16),
            jax.ShapeDtypeStruct((16, 16, PC), BF16),
            jax.ShapeDtypeStruct((32, PC), F32),
        )
        + state,
        in_specs=vmem(10),
        out_specs=tuple(vmem(5)),
        scratch_shapes=[pltpu.VMEM((288, C), BF16)],
        input_output_aliases={8: 3, 9: 4},
        compiler_params=pltpu.CompilerParams(vmem_limit_bytes=16 * 1024 * 1024),
        cost_estimate=pl.CostEstimate(
            flops=1_000_000_000, bytes_accessed=1_000_000, transcendentals=600_000
        ),
        name="outer",
    )(inner, outer, norm_gains, taps, table, point, query_weight, key_weight, x, n)

    own_keys = lax.all_to_all(keys, ("x_hi", "z"), 0, 0, tiled=False)
    other_keys = lax.ppermute(own_keys, "core", [(0, 1), (1, 0)])

    pair_map = pl.pallas_call(
        pair_kernel_body,
        out_shape=jax.ShapeDtypeStruct((16, 512, PC), BF16),
        in_specs=vmem(4),
        out_specs=pl.BlockSpec(memory_space=pl.ANY),
        scratch_shapes=[
            pltpu.VMEM((18, PC, PC), F32),
            pltpu.VMEM((9, PC, PC), F32),
            pltpu.VMEM((512, PC), F32),
            pltpu.VMEM((512, 3 * PC), BF16),
            pltpu.VMEM((16, 512, PC), BF16),
            pltpu.VMEM((3 * PC, 2 * PC), BF16),
            pltpu.SemaphoreType.DMA((8,)),
        ],
        compiler_params=pltpu.CompilerParams(vmem_limit_bytes=24 * 1024 * 1024),
        name="pair",
    )(queries, own_keys, other_keys, pair_kernel)
    return (trunk, pair_map)


def solution(mesh):
    devices = mesh.devices.reshape(2, 8, 2, -1)
    fine = Mesh(devices, ("x_hi", "z", "core", "batch"))
    rows = ("batch", "x_hi", "z", "core")
    return jax.shard_map(
        on_device,
        mesh=fine,
        in_specs=(P(rows, None), P(), P(), P(), P(), P(), P(), P()),
        out_specs=(P(rows, None), P(rows, None, None)),
        check_vma=False,
    )
```

time: 56.2 us -> 42.8 us (0.76)
  local copies, waits for them, and re-layouts: 8.34 us -> 0.02 us
  waiting for transfers between devices: 3.61 us -> 0.91 us
  Pallas kernels: 17.6 us -> 15.8 us
  starting transfers between devices: 7.47 us -> 6.6 us
    unnamed x15 -> x10, local copies, waits for them, and re-layouts: 7.44 us -> 0.02 us
    ppermute x2, waiting for transfers between devices: 2.71 us -> 0.01 us  [the longest x1 0.01 us: on_device(): inner = lax.ppermute(bases, 'core', [(0, 1), (1, 0)])]
    pallas_call x1 -> x2, Pallas kernels: 12.8 us -> 11 us  [the longest x1 5.61 us: on_device(): pl.pallas_call(inner_kernel, out_shape=state + (jax.ShapeDtypeStruct((4 *...]
    dynamic_slice x1 -> x0, local copies, waits for them, and re-layouts: 0.9 us -> none  [on_device(): inner_send = lax.dynamic_slice(bases, (head_first, 0), (HALO, BASES))]
    ppermute x1, starting transfers between devices: 2.28 us -> 1.41 us  [on_device(): other_keys = lax.ppermute(own_keys, 'core', [(0, 1), (1, 0)])]
  transfers between devices with their start and end apart: 3 -> 3, of which waited for: 2 -> 1; matrix products, arithmetic and copies ran while one was open for 2% -> 0% of each run, Pallas kernels for 0% -> 13%
where the time goes in v2:
time: 42.8 us; the launch traced here: 42.6 us
  blocking collectives  18.5 us (43%)
  Pallas kernels  15.8 us (37%)
  starting transfers between devices  6.6 us (15%)
  waiting for transfers between devices  0.91 us (2%)
  between operations  0.74 us (2%)
    all_to_all x1, blocking collectives, on_device(): own_keys = lax.all_to_all(keys, ('x_hi', 'z'), 0, 0, tiled=False)  18.5 us
    pallas_call x1, Pallas kernels, on_device(): pl.pallas_call(inner_kernel, out_shape=state + (jax.ShapeDtypeStruct((4 *...  5.61 us
    pallas_call x1, Pallas kernels, on_device(): pl.pallas_call(outer_kernel, out_shape=(jax.ShapeDtypeStruct((SLAB, C), B...  5.42 us
    pallas_call x1, Pallas kernels, on_device(): pl.pallas_call(pair_kernel_body, out_shape=jax.ShapeDtypeStruct((16, 512,...  4.81 us
    ppermute x1, starting transfers between devices, on_device(): inner = lax.ppermute(bases, 'core', [(0, 1), (1, 0)])  3.29 us
    ppermute x1, starting transfers between devices, on_device(): outer = lax.ppermute(bases, seq, outer_pairs)  1.91 us
    ppermute x1, starting transfers between devices, on_device(): other_keys = lax.ppermute(own_keys, 'core', [(0, 1), (1, 0)])  1.41 us
    ppermute x1, waiting for transfers between devices, on_device(): other_keys = lax.ppermute(own_keys, 'core', [(0, 1), (1, 0)])  0.9 us
  transfers between devices with their start and end apart: 3, of which 1 were waited for; matrix products, arithmetic and copies ran while one was open for 0% of the time, Pallas kernels for 13%

profile of v2, /device:TPU:1, one launch (start us, length us, event | category | flops | bytes accessed | tf_op | source)
XLA Modules:
  0.0 42.6 jit_solution(15508484536880794054)
XLA Ops:
  0.6 0.0 copy-start.4
  0.6 0.0 copy-start.1
  0.7 0.0 copy-start.3
  0.7 0.0 copy-start.2
  0.7 3.3 %collective-permute-start = (s32[256,128]{1,0:T(8,128)}, s32[256,128]{1,0:T(8,128)S(1)}, u32[]{:S(2)}, u32[]{:S(2)}) collective-permute-start(s32[256,128]{1,0:T(8,128)} %own.1), channel_id=1, source_target_pairs={{0,8},{8,0},{1,9},{9,1},{2,10},{10,2},{3,11},{11,3},{4,12},{12,4},... | collective-permute-start | bytes 393224 | tf_op jit(solution)/shard_map/ppermute | solution.py:241
  4.0 1.9 %collective-permute-start.1 = (s32[256,128]{1,0:T(8,128)}, s32[256,128]{1,0:T(8,128)S(1)}, u32[]{:S(2)}, u32[]{:S(2)}) collective-permute-start(s32[256,128]{1,0:T(8,128)} %own.1), channel_id=1, source_target_pairs={{8,16},{16,8},{24,32},{32,24},{40,48},{48,40},{56,64},{64,56},{72,... | collective-permute-start | bytes 393224 | tf_op jit(solution)/shard_map/ppermute | solution.py:242
  5.9 5.6 %inner.1 = (f32[480,768]{1,0:T(8,128)S(1)}, f32[3,6,480,128]{3,2,1,0:T(8,128)S(1)}, bf16[512,768]{1,0:T(8,128)(2,1)S(1)}, bf16[3,768,768]{2,1,0:T(8,128)(2,1)S(1)}) custom-call(s32[256,128]{1,0:T(8,128)} %own.1, bf16[512,768]{1,0:T(8,128)(2,1)} %table_hbm.1, f32[3,768]{1,0:T(4,128)} %gains.3, f32[5,3,768]{2,1,0:T(4,128)} %bitcast.1, ...), custom_call_target="tpu_custom_call" | custom-call | flops 800000000 | bytes 5000000 | tf_op jit(solution)/shard_map/inner/pallas_call | solution.py:250
  11.5 0.0 collective-permute-done.inner
  11.5 0.0 collective-permute-done.1.outer
  11.5 0.0 copy-done.4
  11.5 0.0 copy-done.1
  11.5 0.0 copy-done.3
  11.5 0.0 copy-done.2
  11.6 0.0 copy-start
  11.6 5.4 %outer.1 = (bf16[256,768]{1,0:T(8,128)(2,1)}, bf16[16,16,128]{2,1,0:T(8,128)(2,1)S(1)}, f32[32,128]{1,0:T(8,128)S(1)}, f32[480,768]{1,0:T(8,128)S(1)}, f32[3,6,480,128]{3,2,1,0:T(8,128)S(1)}) custom-call(s32[256,128]{1,0:T(8,128)S(1)} %collective-permute-done.inner, ...), custom_call_target="tpu_custom_call", output_to_operand_aliasing={{3}: (8, {}), {4}: (9, {})} | custom-call | flops 1000000000 | bytes 1000000 | tf_op jit(solution)/shard_map/outer/pallas_call | solution.py:266
  17.0 18.5 %all_to_all.5.own = bf16[16,16,128]{2,1,0:T(8,128)(2,1)S(1)} all-to-all(bf16[16,16,128]{2,1,0:T(8,128)(2,1)S(1)} %get-tuple-element.15), channel_id=1, replica_groups=mesh['x_hi'=2,'z'=8,'core'=2,'batch'=8] {'x_hi','z'}, dimensions={0} | all-to-all | bytes 131072 | tf_op jit(solution)/shard_map/all_to_all | solution.py:285
  35.5 1.4 %collective-permute-start.2 = (bf16[16,16,128]{2,1,0:T(8,128)(2,1)S(1)}, bf16[16,16,128]{2,1,0:T(8,128)(2,1)S(1)}, u32[]{:S(2)}, u32[]{:S(2)}) collective-permute-start(bf16[16,16,128]{2,1,0:T(8,128)(2,1)S(1)} %all_to_all.5.own), channel_id=1, source_target_pairs={{0,8},{8,0},{1,9},{9,1},{2,10},{10,2},{3,11},{11,3},{4,12},{12,4},... | collective-permute-start | bytes 196616 | tf_op jit(solution)/shard_map/ppermute | solution.py:286
  36.9 0.9 %collective-permute-done.2.other = bf16[16,16,128]{2,1,0:T(8,128)(2,1)S(1)} collective-permute-done((bf16[16,16,128]{2,1,0:T(8,128)(2,1)S(1)}, bf16[16,16,128]{2,1,0:T(8,128)(2,1)S(1)}, u32[]{:S(2)}, u32[]{:S(2)}) %collective-permute-start.2) | collective-permute-done | bytes 65568 | tf_op jit(solution)/shard_map/ppermute | solution.py:286
  37.8 0.0 copy-done
  37.8 4.8 %pair.1 = bf16[16,512,128]{2,1,0:T(8,128)(2,1)} custom-call(f32[32,128]{1,0:T(8,128)S(1)} %get-tuple-element.14.queries, bf16[16,16,128]{2,1,0:T(8,128)(2,1)S(1)} %all_to_all.5.own, bf16[16,16,128]{2,1,0:T(8,128)(2,1)S(1)} %collective-permute-done.2.other, bf16[3,3,128,128]{3,2,1,0:T(8,128)(2,1)S(1)} %copy-done), custom_call_target="tpu_custom_call" | custom-call | tf_op jit(solution)/shard_map/pair/pallas_call | solution.py:288
Async XLA Ops:
  0.6 10.9 %copy-start.4 = (f32[3,768]{1,0:T(4,128)S(1)}, f32[3,768]{1,0:T(4,128)}, u32[]{:S(2)}) copy-start(f32[3,768]{1,0:T(4,128)} %gains.3) | copy-start | bytes 27652
  0.6 10.9 %copy-start.1 = (f32[3,5,768]{2,0,1:T(4,128)S(1)}, f32[3,5,768]{2,0,1:T(4,128)}, u32[]{:S(2)}) copy-start(f32[3,5,768]{2,0,1:T(4,128)} %param.11) | copy-start | bytes 138244
  0.7 10.9 %copy-start.3 = (bf16[768,128]{1,0:T(8,128)(2,1)S(1)}, bf16[768,128]{1,0:T(8,128)(2,1)}, u32[]{:S(2)}) copy-start(bf16[768,128]{1,0:T(8,128)(2,1)} %key_w.1) | copy-start | bytes 589828
  0.7 10.9 %copy-start.2 = (bf16[768,128]{1,0:T(8,128)(2,1)S(1)}, bf16[768,128]{1,0:T(8,128)(2,1)}, u32[]{:S(2)}) copy-start(bf16[768,128]{1,0:T(8,128)(2,1)} %query_w.1) | copy-start | bytes 589828
  0.7 10.8 %collective-permute-start = (s32[256,128]{1,0:T(8,128)}, s32[256,128]{1,0:T(8,128)S(1)}, u32[]{:S(2)}, u32[]{:S(2)}) collective-permute-start(s32[256,128]{1,0:T(8,128)} %own.1), channel_id=1, source_target_pairs={{0,8},{8,0},{1,9},{9,1},{2,10},{10,2},{3,11},{11,3},{4,12},{12,4},... | collective-permute-start | bytes 393224 | tf_op jit(solution)/shard_map/ppermute | solution.py:241
  4.0 7.5 %collective-permute-start.1 = (s32[256,128]{1,0:T(8,128)}, s32[256,128]{1,0:T(8,128)S(1)}, u32[]{:S(2)}, u32[]{:S(2)}) collective-permute-start(s32[256,128]{1,0:T(8,128)} %own.1), channel_id=1, source_target_pairs={{8,16},{16,8},{24,32},{32,24},{40,48},{48,40},{56,64},{64,56},{72,... | collective-permute-start | bytes 393224 | tf_op jit(solution)/shard_map/ppermute | solution.py:242
  11.6 26.2 %copy-start = (bf16[3,3,128,128]{3,2,1,0:T(8,128)(2,1)S(1)}, bf16[3,3,128,128]{3,2,1,0:T(8,128)(2,1)}, u32[]{:S(2)}) copy-start(bf16[3,3,128,128]{3,2,1,0:T(8,128)(2,1)} %kernel.1) | copy-start | bytes 884740
  35.5 2.3 %collective-permute-start.2 = (bf16[16,16,128]{2,1,0:T(8,128)(2,1)S(1)}, bf16[16,16,128]{2,1,0:T(8,128)(2,1)S(1)}, u32[]{:S(2)}, u32[]{:S(2)}) collective-permute-start(bf16[16,16,128]{2,1,0:T(8,128)(2,1)S(1)} %all_to_all.5.own), channel_id=1, source_target_pairs={{0,8},{8,0},{1,9},{9,1},{2,10},{10,2},{3,11},{11,3},{4,12},{12,4},... | collective-permute-start | bytes 196616 | tf_op jit(solution)/shard_map/ppermute | solution.py:286

commit v3 on v2

--- a/solution.py
+++ b/solution.py
@@ -26,8 +26,9 @@
 
 
 def gelu_of_half(half):
+    half = half.astype(BF16)
     squared = half * half
-    inner = half * (2.0 * GELU_A + (8.0 * GELU_B) * squared)
+    inner = half * (jnp.asarray(2.0 * GELU_A, BF16) + jnp.asarray(8.0 * GELU_B, BF16) * squared)
     return half + half * jnp.tanh(inner)
 
 
@@ -38,11 +39,10 @@
     ).astype(F32).astype(BF16)
 
 
-def embed(codes, spread, table):
+def one_hot_rows(codes, spread):
     repeated = jnp.dot(codes.astype(F32).astype(BF16), spread, preferred_element_type=F32)
     base = (lax.broadcasted_iota(jnp.int32, repeated.shape, 1) % 4).astype(F32)
-    one_hot = jnp.where(repeated == base, 1.0, 0.0).astype(BF16)
-    return jnp.dot(one_hot, table[...], preferred_element_type=F32)
+    return jnp.where(repeated == base, 1.0, 0.0).astype(BF16)
 
 
 def norm_rows(x_ref, n_ref, layer, count, row_of, scale_of, unroll):
@@ -73,7 +73,7 @@
                 piece = n_ref[layer, c, pl.ds(at + (t - 2) * reach, STEP), :]
                 term = piece * tap_rows[t][:, cols]
                 half = term if half is None else half + term
-            a_ref[pl.ds(to, STEP), cols] = gelu_of_half(half).astype(BF16)
+            a_ref[pl.ds(to, STEP), cols] = gelu_of_half(half)
         return 0
 
     lax.fori_loop(0, count, step, 0, unroll=unroll)
@@ -90,33 +90,44 @@
             done += stop - start
 
 
-def inner_kernel(own, table_hbm, gains, taps, point_hbm, x_ref, n_ref, table, point, a_ref, sems):
-    copies = [pltpu.make_async_copy(table_hbm, table, sems.at[0])]
-    for layer in range(3):
-        copies.append(
-            pltpu.make_async_copy(point_hbm.at[layer], point.at[layer], sems.at[1 + layer])
-        )
+def inner_kernel(
+    own_hbm, table_hbm, gains_hbm, taps_hbm, point_hbm,
+    x_ref, n_ref, table, point,
+    own, gains, taps, a_ref, sems,
+):
+    moves = [(own_hbm, own), (table_hbm, table), (gains_hbm, gains), (taps_hbm, taps)]
+    moves += [(point_hbm.at[layer], point.at[layer]) for layer in range(3)]
+    copies = [
+        pltpu.make_async_copy(source, target, sems.at[k])
+        for k, (source, target) in enumerate(moves)
+    ]
     for copy in copies:
         copy.start()
     spread = spread_matrix()
     copies[0].wait()
     for half in range(2):
-        at = HALO + half * 128
-        x_ref[at : at + 128, :] = embed(own[half * 128 : half * 128 + 128, :], spread, table)
+        rows = slice(half * 128, half * 128 + 128)
+        a_ref[rows, 0 : 4 * BASES] = one_hot_rows(own[rows, :], spread)
+    copies[1].wait()
+    x_ref[HALO : HALO + SLAB, :] = jnp.dot(
+        a_ref[:, 0 : 4 * BASES], table[...], preferred_element_type=F32
+    )
+    copies[2].wait()
+    copies[3].wait()
 
     def one(at):
         return 1.0
 
     norm_rows(x_ref, n_ref, 0, 16, lambda j: HALO + j * STEP, one, 4)
     conv_rows(n_ref, a_ref, 0, gains, taps, 14, lambda j: 128 + j * STEP, 2)
-    copies[1].wait()
+    copies[4].wait()
     mix(a_ref, x_ref, point.at[0], ((128, 352),))
     norm_rows(x_ref, n_ref, 1, 14, lambda j: 128 + j * STEP, one, 7)
     conv_rows(n_ref, a_ref, 1, gains, taps, 12, lambda j: 144 + j * STEP, 2)
-    copies[2].wait()
+    copies[5].wait()
     mix(a_ref, x_ref, point.at[1], ((144, 336),))
     norm_rows(x_ref, n_ref, 2, 12, lambda j: 144 + j * STEP, one, 4)
-    copies[3].wait()
+    copies[6].wait()
 
 
 def outer_kernel(
@@ -129,7 +140,8 @@
     low_bases = jnp.where(core == 0, outer[SLAB - HALO :, :], inner[SLAB - HALO :, :])
     high_bases = jnp.where(core == 0, inner[:HALO, :], outer[:HALO, :])
     spread = spread_matrix()
-    both = embed(jnp.concatenate([low_bases, high_bases], axis=0), spread, table)
+    both = one_hot_rows(jnp.concatenate([low_bases, high_bases], axis=0), spread)
+    both = jnp.dot(both, table[...], preferred_element_type=F32)
     x_ref[0:HALO, :] = both[0:HALO]
     x_ref[HALO + SLAB :, :] = both[HALO:]
 
@@ -168,22 +180,32 @@
         keys_out[peer] = mine
 
 
-def pair_kernel_body(
-    queries, own, other, kernel, out_hbm, wide_q, kernel_f, key_f, key_cat, out_ref, weights, sems
-):
+def weights_kernel(queries, kernel, weights, wide_q):
+    flipped = jnp.transpose(queries[...], (1, 0)) * 0.5
+    for i in range(18):
+        wide_q[i] = jnp.broadcast_to(flipped[:, i : i + 1], (PC, PC)).astype(BF16)
+
+    def two_rows(i, _):
+        for r in range(2):
+            row = 2 * i + r
+            for b in range(3):
+                mixed = wide_q[row] * kernel[0, b]
+                mixed = mixed + wide_q[row + 1] * kernel[1, b]
+                mixed = mixed + wide_q[row + 2] * kernel[2, b]
+                weights[i, b * PC : (b + 1) * PC, r * PC : (r + 1) * PC] = mixed
+        return 0
+
+    lax.fori_loop(0, 8, two_rows, 0)
+
+
+def pair_kernel_body(queries, own, other, weights, out_hbm, key_cat, out_ref, sems):
     core = lax.axis_index("core")
-    flipped = jnp.transpose(queries[...], (1, 0))
-    for i in range(18):
-        wide_q[i] = jnp.broadcast_to(flipped[:, i : i + 1] * 0.5, (PC, PC))
-    for t in range(9):
-        kernel_f[t] = kernel[t // 3, t % 3].astype(F32)
     for g in range(16):
         mine = own[g]
         theirs = other[g]
         key_cat[g * 32 : g * 32 + 16, PC : 2 * PC] = jnp.where(core == 0, mine, theirs)
         key_cat[g * 32 + 16 : g * 32 + 32, PC : 2 * PC] = jnp.where(core == 0, theirs, mine)
     keys = key_cat[:, PC : 2 * PC].astype(F32)
-    key_f[...] = keys
     at = lax.broadcasted_iota(jnp.int32, keys.shape, 0)
     before = jnp.where(at == 0, 0.0, pltpu.roll(keys, 1, 0))
     after = jnp.where(at == 511, 0.0, pltpu.roll(keys, 511, 0))
@@ -196,21 +218,13 @@
         )
 
     def two_rows(i, _):
-        for r in range(2):
-            row = 2 * i + r
-            for b in range(3):
-                mixed = wide_q[row] * kernel_f[b]
-                mixed = mixed + wide_q[row + 1] * kernel_f[3 + b]
-                mixed = mixed + wide_q[row + 2] * kernel_f[6 + b]
-                weights[b * PC : (b + 1) * PC, r * PC : (r + 1) * PC] = mixed.astype(BF16)
-        for m in range(4):
-            rows = slice(m * 128, m * 128 + 128)
-            half = jnp.dot(key_cat[rows, :], weights[...], preferred_element_type=F32)
+        for m in range(2):
+            rows = slice(m * 256, m * 256 + 256)
+            half = jnp.dot(key_cat[rows, :], weights[i], preferred_element_type=F32)
             for r in range(2):
-                query = queries[pl.ds(2 * i + r + 1, 1), :]
-                pair = key_f[rows, :] * query
-                value = pair + gelu_of_half(half[:, r * PC : (r + 1) * PC])
-                out_ref[2 * i + r, rows, :] = value.astype(BF16)
+                query = queries[pl.ds(2 * i + r + 1, 1), :].astype(BF16)
+                pair = key_cat[rows, PC : 2 * PC] * query
+                out_ref[2 * i + r, rows, :] = pair + gelu_of_half(half[:, r * PC : (r + 1) * PC])
         copy_of(i).start()
         return 0
 
@@ -254,9 +268,15 @@
             jax.ShapeDtypeStruct((4 * BASES, C), BF16),
             jax.ShapeDtypeStruct((3, C, C), BF16),
         ),
-        in_specs=vmem(1) + hbm_space + vmem(2) + hbm_space,
+        in_specs=hbm_space * 5,
         out_specs=tuple(vmem(4)),
-        scratch_shapes=[pltpu.VMEM((SLAB, C), BF16), pltpu.SemaphoreType.DMA((4,))],
+        scratch_shapes=[
+            pltpu.VMEM((SLAB, BASES), jnp.int32),
+            pltpu.VMEM((3, C), F32),
+            pltpu.VMEM((5, 3, C), F32),
+            pltpu.VMEM((SLAB, C), BF16),
+            pltpu.SemaphoreType.DMA((7,)),
+        ],
         compiler_params=pltpu.CompilerParams(vmem_limit_bytes=16 * 1024 * 1024),
         cost_estimate=pl.CostEstimate(
             flops=800_000_000, bytes_accessed=5_000_000, transcendentals=400_000
@@ -285,23 +305,31 @@
     own_keys = lax.all_to_all(keys, ("x_hi", "z"), 0, 0, tiled=False)
     other_keys = lax.ppermute(own_keys, "core", [(0, 1), (1, 0)])
 
+    weights = pl.pallas_call(
+        weights_kernel,
+        out_shape=jax.ShapeDtypeStruct((8, 3 * PC, 2 * PC), BF16),
+        in_specs=vmem(2),
+        out_specs=vmem(1)[0],
+        scratch_shapes=[pltpu.VMEM((18, PC, PC), BF16)],
+        compiler_params=pltpu.CompilerParams(vmem_limit_bytes=8 * 1024 * 1024),
+        cost_estimate=pl.CostEstimate(
+            flops=400_000_000, bytes_accessed=2_000_000, transcendentals=0
+        ),
+        name="weights",
+    )(queries, pair_kernel)
     pair_map = pl.pallas_call(
         pair_kernel_body,
         out_shape=jax.ShapeDtypeStruct((16, 512, PC), BF16),
         in_specs=vmem(4),
         out_specs=pl.BlockSpec(memory_space=pl.ANY),
         scratch_shapes=[
-            pltpu.VMEM((18, PC, PC), F32),
-            pltpu.VMEM((9, PC, PC), F32),
-            pltpu.VMEM((512, PC), F32),
             pltpu.VMEM((512, 3 * PC), BF16),
             pltpu.VMEM((16, 512, PC), BF16),
-            pltpu.VMEM((3 * PC, 2 * PC), BF16),
             pltpu.SemaphoreType.DMA((8,)),
         ],
-        compiler_params=pltpu.CompilerParams(vmem_limit_bytes=24 * 1024 * 1024),
+        compiler_params=pltpu.CompilerParams(vmem_limit_bytes=16 * 1024 * 1024),
         name="pair",
-    )(queries, own_keys, other_keys, pair_kernel)
+    )(queries, own_keys, other_keys, weights)
     return (trunk, pair_map)
 
 

time: 42.8 us -> 41.3 us (0.965)
  Pallas kernels: 15.8 us -> 14.7 us
  waiting for transfers between devices: 0.91 us -> 0.03 us
  starting transfers between devices: 6.6 us -> 7.21 us
    pallas_call x0 -> x1, Pallas kernels: none -> 1.12 us  [on_device(): pl.pallas_call(weights_kernel, out_shape=jax.ShapeDtypeStruct((8, 3 * PC,...]
    pallas_call x1, Pallas kernels: 5.61 us -> 4.52 us  [on_device(): pl.pallas_call(inner_kernel, out_shape=state + (jax.ShapeDtypeStruct((4 *...]
    pallas_call x1, Pallas kernels: 4.81 us -> 3.86 us  [on_device(): pl.pallas_call(pair_kernel_body, out_shape=jax.ShapeDtypeStruct((16, 512,...]
    ppermute x1, waiting for transfers between devices: 0.9 us -> 0.01 us  [on_device(): other_keys = lax.ppermute(own_keys, 'core', [(0, 1), (1, 0)])]
    ppermute x1, starting transfers between devices: 1.41 us -> 2.02 us  [on_device(): other_keys = lax.ppermute(own_keys, 'core', [(0, 1), (1, 0)])]
  transfers between devices with their start and end apart: 3 -> 3, of which waited for: 1 -> 0; matrix products, arithmetic and copies ran while one was open for 0% -> 0% of each run, Pallas kernels for 13% -> 14%
where the time goes in v3:
time: 41.3 us; the launch traced here: 41.2 us
  blocking collectives  18.5 us (45%)
  Pallas kernels  14.7 us (36%)
  starting transfers between devices  7.21 us (17%)
  between operations  0.73 us (2%)
    all_to_all x1, blocking collectives, on_device(): own_keys = lax.all_to_all(keys, ('x_hi', 'z'), 0, 0, tiled=False)  18.5 us
    pallas_call x1, Pallas kernels, on_device(): pl.pallas_call(outer_kernel, out_shape=(jax.ShapeDtypeStruct((SLAB, C), B...  5.22 us
    pallas_call x1, Pallas kernels, on_device(): pl.pallas_call(inner_kernel, out_shape=state + (jax.ShapeDtypeStruct((4 *...  4.52 us
    pallas_call x1, Pallas kernels, on_device(): pl.pallas_call(pair_kernel_body, out_shape=jax.ShapeDtypeStruct((16, 512,...  3.86 us
    ppermute x1, starting transfers between devices, on_device(): inner = lax.ppermute(bases, 'core', [(0, 1), (1, 0)])  3.29 us
    ppermute x1, starting transfers between devices, on_device(): other_keys = lax.ppermute(own_keys, 'core', [(0, 1), (1, 0)])  2.02 us
    ppermute x1, starting transfers between devices, on_device(): outer = lax.ppermute(bases, seq, outer_pairs)  1.91 us
    pallas_call x1, Pallas kernels, on_device(): pl.pallas_call(weights_kernel, out_shape=jax.ShapeDtypeStruct((8, 3 * PC,...  1.12 us
  transfers between devices with their start and end apart: 3, of which 0 were waited for; matrix products, arithmetic and copies ran while one was open for 0% of the time, Pallas kernels for 14%

profile of v3, /device:TPU:1, one launch (start us, length us, event | category | flops | bytes accessed | tf_op | source)
XLA Modules:
  0.0 41.2 jit_solution(11239281604241600000)
XLA Ops:
  0.6 0.0 copy-start.4
  0.6 0.0 copy-start.1
  0.7 0.0 copy-start.3
  0.7 0.0 copy-start.2
  0.7 3.3 %collective-permute-start = (s32[256,128]{1,0:T(8,128)}, s32[256,128]{1,0:T(8,128)S(1)}, u32[]{:S(2)}, u32[]{:S(2)}) collective-permute-start(s32[256,128]{1,0:T(8,128)} %own_hbm.1), channel_id=1, source_target_pairs={{0,8},{8,0},{1,9},{9,1},{2,10},{10,2},{3,11},{11,3},{4,12},{12,4},... | collective-permute-start | bytes 393224 | tf_op jit(solution)/shard_map/ppermute | solution.py:255
  4.0 1.9 %collective-permute-start.1 = (s32[256,128]{1,0:T(8,128)}, s32[256,128]{1,0:T(8,128)S(1)}, u32[]{:S(2)}, u32[]{:S(2)}) collective-permute-start(s32[256,128]{1,0:T(8,128)} %own_hbm.1), channel_id=1, source_target_pairs={{8,16},{16,8},{24,32},{32,24},{40,48},{48,40},{56,64},{64,56},{72,... | collective-permute-start | bytes 393224 | tf_op jit(solution)/shard_map/ppermute | solution.py:256
  5.9 4.5 %inner.1 = (f32[480,768]{1,0:T(8,128)S(1)}, f32[3,6,480,128]{3,2,1,0:T(8,128)S(1)}, bf16[512,768]{1,0:T(8,128)(2,1)S(1)}, bf16[3,768,768]{2,1,0:T(8,128)(2,1)S(1)}) custom-call(s32[256,128]{1,0:T(8,128)} %own_hbm.1, bf16[512,768]{1,0:T(8,128)(2,1)} %table_hbm.1, f32[3,768]{1,0:T(4,128)} %gains.1, f32[5,3,768]{2,1,0:T(4,128)} %bitcast.1, ...), custom_call_target="tpu_custom_call" | custom-call | flops 800000000 | bytes 5000000 | tf_op jit(solution)/shard_map/inner/pallas_call | solution.py:264
  10.4 0.0 collective-permute-done.inner
  10.4 0.0 collective-permute-done.1.outer
  10.4 0.0 copy-done.4
  10.4 0.0 copy-done.1
  10.4 0.0 copy-done.3
  10.5 0.0 copy-done.2
  10.5 0.0 copy-start
  10.5 5.2 %outer.1 = (bf16[256,768]{1,0:T(8,128)(2,1)}, bf16[16,16,128]{2,1,0:T(8,128)(2,1)S(1)}, f32[32,128]{1,0:T(8,128)S(1)}, f32[480,768]{1,0:T(8,128)S(1)}, f32[3,6,480,128]{3,2,1,0:T(8,128)S(1)}) custom-call(s32[256,128]{1,0:T(8,128)S(1)} %collective-permute-done.inner, ...), custom_call_target="tpu_custom_call", output_to_operand_aliasing={{3}: (8, {}), {4}: (9, {})} | custom-call | flops 1000000000 | bytes 1000000 | tf_op jit(solution)/shard_map/outer/pallas_call | solution.py:286
  15.7 18.5 %all_to_all.5.own = bf16[16,16,128]{2,1,0:T(8,128)(2,1)S(1)} all-to-all(bf16[16,16,128]{2,1,0:T(8,128)(2,1)S(1)} %get-tuple-element.15), channel_id=1, replica_groups=mesh['x_hi'=2,'z'=8,'core'=2,'batch'=8] {'x_hi','z'}, dimensions={0} | all-to-all | bytes 131072 | tf_op jit(solution)/shard_map/all_to_all | solution.py:305
  34.2 2.0 %collective-permute-start.2 = (bf16[16,16,128]{2,1,0:T(8,128)(2,1)S(1)}, bf16[16,16,128]{2,1,0:T(8,128)(2,1)S(1)}, u32[]{:S(2)}, u32[]{:S(2)}) collective-permute-start(bf16[16,16,128]{2,1,0:T(8,128)(2,1)S(1)} %all_to_all.5.own), channel_id=1, source_target_pairs={{0,8},{8,0},{1,9},{9,1},{2,10},{10,2},{3,11},{11,3},{4,12},{12,4},... | collective-permute-start | bytes 196616 | tf_op jit(solution)/shard_map/ppermute | solution.py:306
  36.2 0.0 copy-done
  36.2 1.1 %weights.1 = bf16[8,384,256]{2,1,0:T(8,128)(2,1)S(1)} custom-call(f32[32,128]{1,0:T(8,128)S(1)} %get-tuple-element.14.queries, bf16[3,3,128,128]{3,2,1,0:T(8,128)(2,1)S(1)} %copy-done), custom_call_target="tpu_custom_call" | custom-call | flops 400000000 | bytes 2000000 | tf_op jit(solution)/shard_map/weights/pallas_call | solution.py:308
  37.3 0.0 collective-permute-done.2.other
  37.3 3.9 %pair.1 = bf16[16,512,128]{2,1,0:T(8,128)(2,1)} custom-call(f32[32,128]{1,0:T(8,128)S(1)} %get-tuple-element.14.queries, bf16[16,16,128]{2,1,0:T(8,128)(2,1)S(1)} %all_to_all.5.own, bf16[16,16,128]{2,1,0:T(8,128)(2,1)S(1)} %collective-permute-done.2.other, bf16[8,384,256]{2,1,0:T(8,128)(2,1)S(1)} %weights.1), custom_call_target="tpu_custom_call" | custom-call | tf_op jit(solution)/shard_map/pair/pallas_call | solution.py:320
Async XLA Ops:
  0.6 9.8 %copy-start.4 = (f32[3,768]{1,0:T(4,128)S(1)}, f32[3,768]{1,0:T(4,128)}, u32[]{:S(2)}) copy-start(f32[3,768]{1,0:T(4,128)} %gains.1) | copy-start | bytes 27652
  0.6 9.8 %copy-start.1 = (f32[3,5,768]{2,0,1:T(4,128)S(1)}, f32[3,5,768]{2,0,1:T(4,128)}, u32[]{:S(2)}) copy-start(f32[3,5,768]{2,0,1:T(4,128)} %param.11) | copy-start | bytes 138244
  0.7 9.8 %copy-start.3 = (bf16[768,128]{1,0:T(8,128)(2,1)S(1)}, bf16[768,128]{1,0:T(8,128)(2,1)}, u32[]{:S(2)}) copy-start(bf16[768,128]{1,0:T(8,128)(2,1)} %key_w.1) | copy-start | bytes 589828
  0.7 9.8 %copy-start.2 = (bf16[768,128]{1,0:T(8,128)(2,1)S(1)}, bf16[768,128]{1,0:T(8,128)(2,1)}, u32[]{:S(2)}) copy-start(bf16[768,128]{1,0:T(8,128)(2,1)} %query_w.1) | copy-start | bytes 589828
  0.7 9.7 %collective-permute-start = (s32[256,128]{1,0:T(8,128)}, s32[256,128]{1,0:T(8,128)S(1)}, u32[]{:S(2)}, u32[]{:S(2)}) collective-permute-start(s32[256,128]{1,0:T(8,128)} %own_hbm.1), channel_id=1, source_target_pairs={{0,8},{8,0},{1,9},{9,1},{2,10},{10,2},{3,11},{11,3},{4,12},{12,4},... | collective-permute-start | bytes 393224 | tf_op jit(solution)/shard_map/ppermute | solution.py:255
  4.0 6.5 %collective-permute-start.1 = (s32[256,128]{1,0:T(8,128)}, s32[256,128]{1,0:T(8,128)S(1)}, u32[]{:S(2)}, u32[]{:S(2)}) collective-permute-start(s32[256,128]{1,0:T(8,128)} %own_hbm.1), channel_id=1, source_target_pairs={{8,16},{16,8},{24,32},{32,24},{40,48},{48,40},{56,64},{64,56},{72,... | collective-permute-start | bytes 393224 | tf_op jit(solution)/shard_map/ppermute | solution.py:256
  10.5 25.7 %copy-start = (bf16[3,3,128,128]{3,2,1,0:T(8,128)(2,1)S(1)}, bf16[3,3,128,128]{3,2,1,0:T(8,128)(2,1)}, u32[]{:S(2)}) copy-start(bf16[3,3,128,128]{3,2,1,0:T(8,128)(2,1)} %kernel.1) | copy-start | bytes 884740
  34.2 3.2 %collective-permute-start.2 = (bf16[16,16,128]{2,1,0:T(8,128)(2,1)S(1)}, bf16[16,16,128]{2,1,0:T(8,128)(2,1)S(1)}, u32[]{:S(2)}, u32[]{:S(2)}) collective-permute-start(bf16[16,16,128]{2,1,0:T(8,128)(2,1)S(1)} %all_to_all.5.own), channel_id=1, source_target_pairs={{0,8},{8,0},{1,9},{9,1},{2,10},{10,2},{3,11},{11,3},{4,12},{12,4},... | collective-permute-start | bytes 196616 | tf_op jit(solution)/shard_map/ppermute | solution.py:306

commit v4 on v3

--- a/solution.py
+++ b/solution.py
@@ -45,55 +45,56 @@
     return jnp.where(repeated == base, 1.0, 0.0).astype(BF16)
 
 
-def norm_rows(x_ref, n_ref, layer, count, row_of, scale_of, unroll):
-    def step(j, _):
-        at = pl.multiple_of(row_of(j), STEP)
-        rows = x_ref[pl.ds(at, STEP), :]
+def norm_rows(x_ref, n_ref, layer, start, stop, scale=None):
+    for at in range(start, stop, STEP):
+        rows = x_ref[at : at + STEP, :]
         mean = jnp.sum(rows * rows, axis=-1, keepdims=True) * (1.0 / C)
-        rows = rows * (lax.rsqrt(mean + 1e-06) * scale_of(at))
+        factor = lax.rsqrt(mean + 1e-06)
+        if scale is not None:
+            factor = factor * scale
+        rows = rows * factor
         for c in range(C // 128):
-            n_ref[layer, c, pl.ds(at, STEP), :] = rows[:, c * 128 : (c + 1) * 128]
-        return 0
-
-    lax.fori_loop(0, count, step, 0, unroll=unroll)
-
-
-def conv_rows(n_ref, a_ref, layer, gains, taps, count, row_of, unroll):
+            n_ref[layer, c, at : at + STEP, :] = rows[:, c * 128 : (c + 1) * 128]
+
+
+def spread_taps(taps, gains, wide_taps):
+    for layer in range(3):
+        gain = gains[layer : layer + 1, :] * 0.5
+        for t in range(5):
+            row = taps[t, layer : layer + 1, :] * gain
+            wide_taps[layer, t] = jnp.broadcast_to(row, (8, C))
+
+
+def conv_rows(n_ref, a_ref, layer, wide_taps, start, stop, to):
     reach = DILATIONS[layer]
-    gain = gains[layer : layer + 1, :] * 0.5
-    tap_rows = [taps[t, layer : layer + 1, :] * gain for t in range(5)]
-
-    def step(j, _):
-        at = row_of(j)
-        to = pl.multiple_of(j * STEP, STEP)
+    for at in range(start, stop, STEP):
         for c in range(C // 128):
             cols = slice(c * 128, (c + 1) * 128)
-            half = None
-            for t in range(5):
-                piece = n_ref[layer, c, pl.ds(at + (t - 2) * reach, STEP), :]
-                term = piece * tap_rows[t][:, cols]
-                half = term if half is None else half + term
-            a_ref[pl.ds(to, STEP), cols] = gelu_of_half(half)
-        return 0
-
-    lax.fori_loop(0, count, step, 0, unroll=unroll)
-
-
-def mix(a_ref, x_ref, weights, spans):
-    total = sum(stop - start for start, stop in spans)
+            halves = []
+            for row in (at, at + 8):
+                half = None
+                for t in range(5):
+                    low = row + (t - 2) * reach
+                    term = n_ref[layer, c, low : low + 8, :] * wide_taps[layer, t, :, cols]
+                    half = term if half is None else half + term
+                halves.append(half)
+            half = jnp.concatenate(halves, axis=0)
+            a_ref[to + at - start : to + at - start + STEP, cols] = gelu_of_half(half)
+
+
+def mix(a_ref, x_ref, weights, start, stop, at):
     for strip in range(3):
         cols = slice(strip * 256, strip * 256 + 256)
-        update = jnp.dot(a_ref[0:total, :], weights[:, cols], preferred_element_type=F32)
-        done = 0
-        for start, stop in spans:
-            x_ref[start:stop, cols] = x_ref[start:stop, cols] + update[done : done + stop - start]
-            done += stop - start
+        update = jnp.dot(
+            a_ref[at : at + stop - start, :], weights[:, cols], preferred_element_type=F32
+        )
+        x_ref[start:stop, cols] = x_ref[start:stop, cols] + update
 
 
 def inner_kernel(
     own_hbm, table_hbm, gains_hbm, taps_hbm, point_hbm,
     x_ref, n_ref, table, point,
-    own, gains, taps, a_ref, sems,
+    own, gains, taps, wide_taps, a_ref, sems,
 ):
     moves = [(own_hbm, own), (table_hbm, table), (gains_hbm, gains), (taps_hbm, taps)]
     moves += [(point_hbm.at[layer], point.at[layer]) for layer in range(3)]
@@ -114,25 +115,21 @@
     )
     copies[2].wait()
     copies[3].wait()
-
-    def one(at):
-        return 1.0
-
-    norm_rows(x_ref, n_ref, 0, 16, lambda j: HALO + j * STEP, one, 4)
-    conv_rows(n_ref, a_ref, 0, gains, taps, 14, lambda j: 128 + j * STEP, 2)
-    copies[4].wait()
-    mix(a_ref, x_ref, point.at[0], ((128, 352),))
-    norm_rows(x_ref, n_ref, 1, 14, lambda j: 128 + j * STEP, one, 7)
-    conv_rows(n_ref, a_ref, 1, gains, taps, 12, lambda j: 144 + j * STEP, 2)
-    copies[5].wait()
-    mix(a_ref, x_ref, point.at[1], ((144, 336),))
-    norm_rows(x_ref, n_ref, 2, 12, lambda j: 144 + j * STEP, one, 4)
+    spread_taps(taps, gains, wide_taps)
+    norm_rows(x_ref, n_ref, 0, 112, 368)
+    for layer, low, high in ((0, 128, 352), (1, 144, 336)):
+        copies[4 + layer].wait()
+        middle = (low + high) // 2
+        for start, stop in ((low, middle), (middle, high)):
+            conv_rows(n_ref, a_ref, layer, wide_taps, start, stop, start - low)
+            mix(a_ref, x_ref, point.at[layer], start, stop, start - low)
+            norm_rows(x_ref, n_ref, layer + 1, start, stop)
     copies[6].wait()
 
 
 def outer_kernel(
     inner, outer, gains, taps, table, point, query_w, key_w, x_in, n_in,
-    trunk_out, keys_out, query_out, x_ref, n_ref, a_ref,
+    trunk_out, keys_out, query_out, x_ref, n_ref, wide_taps, a_ref,
 ):
     del x_in, n_in
     place = lax.axis_index(("x_hi", "z", "core"))
@@ -140,27 +137,33 @@
     low_bases = jnp.where(core == 0, outer[SLAB - HALO :, :], inner[SLAB - HALO :, :])
     high_bases = jnp.where(core == 0, inner[:HALO, :], outer[:HALO, :])
     spread = spread_matrix()
-    both = one_hot_rows(jnp.concatenate([low_bases, high_bases], axis=0), spread)
-    both = jnp.dot(both, table[...], preferred_element_type=F32)
-    x_ref[0:HALO, :] = both[0:HALO]
-    x_ref[HALO + SLAB :, :] = both[HALO:]
-
-    def inside(at):
-        gone = ((at < HALO) & (place == 0)) | ((at >= HALO + SLAB) & (place == 31))
-        return jnp.where(gone, 0.0, 1.0)
-
-    def two_spans(low, high):
-        return lambda j: jnp.where(j < 7, low + j * STEP, high + (j - 7) * STEP)
-
-    norm_rows(x_ref, n_ref, 0, 14, two_spans(0, 368), inside, 7)
-    conv_rows(n_ref, a_ref, 0, gains, taps, 14, two_spans(16, 352), 2)
-    mix(a_ref, x_ref, point.at[0], ((16, 128), (352, 464)))
-    norm_rows(x_ref, n_ref, 1, 14, two_spans(16, 352), inside, 7)
-    conv_rows(n_ref, a_ref, 1, gains, taps, 14, two_spans(32, 336), 2)
-    mix(a_ref, x_ref, point.at[1], ((32, 144), (336, 448)))
-    norm_rows(x_ref, n_ref, 2, 14, two_spans(32, 336), inside, 7)
-    conv_rows(n_ref, a_ref, 2, gains, taps, 18, lambda j: 96 + j * STEP, 2)
-    mix(a_ref, x_ref, point.at[2], ((96, 384),))
+    a_ref[0:HALO, 0 : 4 * BASES] = one_hot_rows(low_bases, spread)
+    a_ref[HALO : 2 * HALO, 0 : 4 * BASES] = one_hot_rows(high_bases, spread)
+    x_ref[0:HALO, :] = jnp.dot(
+        a_ref[0:HALO, 0 : 4 * BASES], table[...], preferred_element_type=F32
+    )
+    x_ref[HALO + SLAB :, :] = jnp.dot(
+        a_ref[HALO : 2 * HALO, 0 : 4 * BASES], table[...], preferred_element_type=F32
+    )
+    spread_taps(taps, gains, wide_taps)
+    low_scale = jnp.where(place == 0, 0.0, 1.0)
+    high_scale = jnp.where(place == 31, 0.0, 1.0)
+
+    norm_rows(x_ref, n_ref, 0, 0, 112, low_scale)
+    norm_rows(x_ref, n_ref, 0, 368, 480, high_scale)
+    for layer, reach_out in ((0, 0), (1, 16)):
+        low, high = 16 + reach_out, 352 - reach_out
+        conv_rows(n_ref, a_ref, layer, wide_taps, low, low + 112, 0)
+        mix(a_ref, x_ref, point.at[layer], low, low + 112, 0)
+        norm_rows(x_ref, n_ref, layer + 1, low, 112, low_scale)
+        norm_rows(x_ref, n_ref, layer + 1, 112, low + 112)
+        conv_rows(n_ref, a_ref, layer, wide_taps, high, high + 112, 112)
+        mix(a_ref, x_ref, point.at[layer], high, high + 112, 112)
+        norm_rows(x_ref, n_ref, layer + 1, high, 368)
+        norm_rows(x_ref, n_ref, layer + 1, 368, high + 112, high_scale)
+    for start, stop in ((96, 240), (240, 384)):
+        conv_rows(n_ref, a_ref, 2, wide_taps, start, stop, start - 96)
+        mix(a_ref, x_ref, point.at[2], start, stop, start - 96)
 
     trunk = x_ref[96:384, :].astype(BF16)
     trunk_out[...] = trunk[POOL : POOL + SLAB, :]
@@ -198,7 +201,7 @@
     lax.fori_loop(0, 8, two_rows, 0)
 
 
-def pair_kernel_body(queries, own, other, weights, out_hbm, key_cat, out_ref, sems):
+def pair_kernel_body(queries, own, other, weights, out_hbm, key_cat, key_f, out_ref, sems):
     core = lax.axis_index("core")
     for g in range(16):
         mine = own[g]
@@ -206,6 +209,7 @@
         key_cat[g * 32 : g * 32 + 16, PC : 2 * PC] = jnp.where(core == 0, mine, theirs)
         key_cat[g * 32 + 16 : g * 32 + 32, PC : 2 * PC] = jnp.where(core == 0, theirs, mine)
     keys = key_cat[:, PC : 2 * PC].astype(F32)
+    key_f[...] = keys
     at = lax.broadcasted_iota(jnp.int32, keys.shape, 0)
     before = jnp.where(at == 0, 0.0, pltpu.roll(keys, 1, 0))
     after = jnp.where(at == 511, 0.0, pltpu.roll(keys, 511, 0))
@@ -217,18 +221,16 @@
             out_ref.at[pl.ds(2 * i, 2)], out_hbm.at[pl.ds(2 * i, 2)], sems.at[i]
         )
 
-    def two_rows(i, _):
+    for i in range(8):
+        query_rows = [queries[2 * i + r + 1 : 2 * i + r + 2, :].astype(BF16) for r in range(2)]
         for m in range(2):
             rows = slice(m * 256, m * 256 + 256)
             half = jnp.dot(key_cat[rows, :], weights[i], preferred_element_type=F32)
+            key = key_f[rows, :].astype(BF16)
             for r in range(2):
-                query = queries[pl.ds(2 * i + r + 1, 1), :].astype(BF16)
-                pair = key_cat[rows, PC : 2 * PC] * query
-                out_ref[2 * i + r, rows, :] = pair + gelu_of_half(half[:, r * PC : (r + 1) * PC])
+                gelu = gelu_of_half(half[:, r * PC : (r + 1) * PC])
+                out_ref[2 * i + r, rows, :] = key * query_rows[r] + gelu
         copy_of(i).start()
-        return 0
-
-    lax.fori_loop(0, 8, two_rows, 0)
 
     def finish(i, _):
         copy_of(i).wait()
@@ -274,6 +276,7 @@
             pltpu.VMEM((SLAB, BASES), jnp.int32),
             pltpu.VMEM((3, C), F32),
             pltpu.VMEM((5, 3, C), F32),
+            pltpu.VMEM((3, 5, 8, C), F32),
             pltpu.VMEM((SLAB, C), BF16),
             pltpu.SemaphoreType.DMA((7,)),
         ],
@@ -293,7 +296,7 @@
         + state,
         in_specs=vmem(10),
         out_specs=tuple(vmem(5)),
-        scratch_shapes=[pltpu.VMEM((288, C), BF16)],
+        scratch_shapes=[pltpu.VMEM((3, 5, 8, C), F32), pltpu.VMEM((288, C), BF16)],
         input_output_aliases={8: 3, 9: 4},
         compiler_params=pltpu.CompilerParams(vmem_limit_bytes=16 * 1024 * 1024),
         cost_estimate=pl.CostEstimate(
@@ -324,6 +327,7 @@
         out_specs=pl.BlockSpec(memory_space=pl.ANY),
         scratch_shapes=[
             pltpu.VMEM((512, 3 * PC), BF16),
+            pltpu.VMEM((512, PC), F32),
             pltpu.VMEM((16, 512, PC), BF16),
             pltpu.SemaphoreType.DMA((8,)),
         ],

time: 41.3 us -> 38.2 us (0.925)
  Pallas kernels: 14.7 us -> 10.5 us
  waiting for transfers between devices: 0.03 us -> 1.12 us
  blocking collectives: 18.5 us -> 18 us
  starting transfers between devices: 7.21 us -> 7.7 us
    pallas_call x1, Pallas kernels: 3.86 us -> 2.16 us  [on_device(): pl.pallas_call(pair_kernel_body, out_shape=jax.ShapeDtypeStruct((16, 512,...]
    pallas_call x1, Pallas kernels: 5.22 us -> 3.74 us  [on_device(): pl.pallas_call(outer_kernel, out_shape=(jax.ShapeDtypeStruct((SLAB, C), B...]
    ppermute x1, waiting for transfers between devices: 0.03 us -> 1.12 us  [on_device(): outer = lax.ppermute(bases, seq, outer_pairs)]
    pallas_call x1, Pallas kernels: 4.52 us -> 3.43 us  [on_device(): pl.pallas_call(inner_kernel, out_shape=state + (jax.ShapeDtypeStruct((4 *...]
    ppermute x1, starting transfers between devices: 2.02 us -> 2.5 us  [on_device(): other_keys = lax.ppermute(own_keys, 'core', [(0, 1), (1, 0)])]
    all_to_all x1, blocking collectives: 18.5 us -> 18 us  [on_device(): own_keys = lax.all_to_all(keys, ('x_hi', 'z'), 0, 0, tiled=False)]
  transfers between devices with their start and end apart: 3 -> 3, of which waited for: 0 -> 1; matrix products, arithmetic and copies ran while one was open for 0% -> 0% of each run, Pallas kernels for 14% -> 12%
where the time goes in v4:
time: 38.2 us; the launch traced here: 38 us
  blocking collectives  18 us (47%)
  Pallas kernels  10.5 us (27%)
  starting transfers between devices  7.7 us (20%)
  waiting for transfers between devices  1.12 us (3%)
  between operations  0.73 us (2%)
    all_to_all x1, blocking collectives, on_device(): own_keys = lax.all_to_all(keys, ('x_hi', 'z'), 0, 0, tiled=False)  18 us
    pallas_call x1, Pallas kernels, on_device(): pl.pallas_call(outer_kernel, out_shape=(jax.ShapeDtypeStruct((SLAB, C), B...  3.74 us
    pallas_call x1, Pallas kernels, on_device(): pl.pallas_call(inner_kernel, out_shape=state + (jax.ShapeDtypeStruct((4 *...  3.43 us
    ppermute x1, starting transfers between devices, on_device(): inner = lax.ppermute(bases, 'core', [(0, 1), (1, 0)])  3.29 us
    ppermute x1, starting transfers between devices, on_device(): other_keys = lax.ppermute(own_keys, 'core', [(0, 1), (1, 0)])  2.5 us
    pallas_call x1, Pallas kernels, on_device(): pl.pallas_call(pair_kernel_body, out_shape=jax.ShapeDtypeStruct((16, 512,...  2.16 us
    ppermute x1, starting transfers between devices, on_device(): outer = lax.ppermute(bases, seq, outer_pairs)  1.91 us
    pallas_call x1, Pallas kernels, on_device(): pl.pallas_call(weights_kernel, out_shape=jax.ShapeDtypeStruct((8, 3 * PC,...  1.12 us
  transfers between devices with their start and end apart: 3, of which 1 were waited for; matrix products, arithmetic and copies ran while one was open for 0% of the time, Pallas kernels for 12%

profile of v4, /device:TPU:1, one launch (start us, length us, event | category | flops | bytes accessed | tf_op | source)
XLA Modules:
  0.0 38.0 jit_solution(7908548260084152437)
XLA Ops:
  0.6 0.0 copy-start.4
  0.6 0.0 copy-start.1
  0.7 0.0 copy-start.3
  0.7 0.0 copy-start.2
  0.7 3.3 %collective-permute-start = (s32[256,128]{1,0:T(8,128)}, s32[256,128]{1,0:T(8,128)S(1)}, u32[]{:S(2)}, u32[]{:S(2)}) collective-permute-start(s32[256,128]{1,0:T(8,128)} %own_hbm.1), channel_id=1, source_target_pairs={{0,8},{8,0},{1,9},{9,1},{2,10},{10,2},{3,11},{11,3},{4,12},{12,4},... | collective-permute-start | bytes 393224 | tf_op jit(solution)/shard_map/ppermute | solution.py:257
  4.0 1.9 %collective-permute-start.1 = (s32[256,128]{1,0:T(8,128)}, s32[256,128]{1,0:T(8,128)S(1)}, u32[]{:S(2)}, u32[]{:S(2)}) collective-permute-start(s32[256,128]{1,0:T(8,128)} %own_hbm.1), channel_id=1, source_target_pairs={{8,16},{16,8},{24,32},{32,24},{40,48},{48,40},{56,64},{64,56},{72,... | collective-permute-start | bytes 393224 | tf_op jit(solution)/shard_map/ppermute | solution.py:258
  5.9 3.4 %inner.1 = (f32[480,768]{1,0:T(8,128)S(1)}, f32[3,6,480,128]{3,2,1,0:T(8,128)S(1)}, bf16[512,768]{1,0:T(8,128)(2,1)S(1)}, bf16[3,768,768]{2,1,0:T(8,128)(2,1)S(1)}) custom-call(s32[256,128]{1,0:T(8,128)} %own_hbm.1, bf16[512,768]{1,0:T(8,128)(2,1)} %table_hbm.1, f32[3,768]{1,0:T(4,128)} %gains.1, f32[5,3,768]{2,1,0:T(4,128)} %bitcast.1, ...), custom_call_target="tpu_custom_call" | custom-call | flops 800000000 | bytes 5000000 | tf_op jit(solution)/shard_map/inner/pallas_call | solution.py:266
  9.3 0.0 collective-permute-done.inner
  9.3 1.1 %collective-permute-done.1.outer = s32[256,128]{1,0:T(8,128)S(1)} collective-permute-done((s32[256,128]{1,0:T(8,128)}, s32[256,128]{1,0:T(8,128)S(1)}, u32[]{:S(2)}, u32[]{:S(2)}) %collective-permute-start.1) | collective-permute-done | bytes 131104 | tf_op jit(solution)/shard_map/ppermute | solution.py:258
  10.4 0.0 copy-done.4
  10.4 0.0 copy-done.1
  10.4 0.0 copy-done.3
  10.5 0.0 copy-done.2
  10.5 0.0 copy-start
  10.5 3.7 %outer.1 = (bf16[256,768]{1,0:T(8,128)(2,1)}, bf16[16,16,128]{2,1,0:T(8,128)(2,1)S(1)}, f32[32,128]{1,0:T(8,128)S(1)}, f32[480,768]{1,0:T(8,128)S(1)}, f32[3,6,480,128]{3,2,1,0:T(8,128)S(1)}) custom-call(s32[256,128]{1,0:T(8,128)S(1)} %collective-permute-done.inner, ...), custom_call_target="tpu_custom_call", output_to_operand_aliasing={{3}: (8, {}), {4}: (9, {})} | custom-call | flops 1000000000 | bytes 1000000 | tf_op jit(solution)/shard_map/outer/pallas_call | solution.py:289
  14.2 18.0 %all_to_all.5.own = bf16[16,16,128]{2,1,0:T(8,128)(2,1)S(1)} all-to-all(bf16[16,16,128]{2,1,0:T(8,128)(2,1)S(1)} %get-tuple-element.15), channel_id=1, replica_groups=mesh['x_hi'=2,'z'=8,'core'=2,'batch'=8] {'x_hi','z'}, dimensions={0} | all-to-all | bytes 131072 | tf_op jit(solution)/shard_map/all_to_all | solution.py:308
  32.2 2.5 %collective-permute-start.2 = (bf16[16,16,128]{2,1,0:T(8,128)(2,1)S(1)}, bf16[16,16,128]{2,1,0:T(8,128)(2,1)S(1)}, u32[]{:S(2)}, u32[]{:S(2)}) collective-permute-start(bf16[16,16,128]{2,1,0:T(8,128)(2,1)S(1)} %all_to_all.5.own), channel_id=1, source_target_pairs={{0,8},{8,0},{1,9},{9,1},{2,10},{10,2},{3,11},{11,3},{4,12},{12,4},... | collective-permute-start | bytes 196616 | tf_op jit(solution)/shard_map/ppermute | solution.py:309
  34.7 0.0 copy-done
  34.7 1.1 %weights.1 = bf16[8,384,256]{2,1,0:T(8,128)(2,1)S(1)} custom-call(f32[32,128]{1,0:T(8,128)S(1)} %get-tuple-element.14.queries, bf16[3,3,128,128]{3,2,1,0:T(8,128)(2,1)S(1)} %copy-done), custom_call_target="tpu_custom_call" | custom-call | flops 400000000 | bytes 2000000 | tf_op jit(solution)/shard_map/weights/pallas_call | solution.py:311
  35.9 0.0 collective-permute-done.2.other
  35.9 2.2 %pair.1 = bf16[16,512,128]{2,1,0:T(8,128)(2,1)} custom-call(f32[32,128]{1,0:T(8,128)S(1)} %get-tuple-element.14.queries, bf16[16,16,128]{2,1,0:T(8,128)(2,1)S(1)} %all_to_all.5.own, bf16[16,16,128]{2,1,0:T(8,128)(2,1)S(1)} %collective-permute-done.2.other, bf16[8,384,256]{2,1,0:T(8,128)(2,1)S(1)} %weights.1), custom_call_target="tpu_custom_call" | custom-call | tf_op jit(solution)/shard_map/pair/pallas_call | solution.py:323
Async XLA Ops:
  0.6 9.8 %copy-start.4 = (f32[3,768]{1,0:T(4,128)S(1)}, f32[3,768]{1,0:T(4,128)}, u32[]{:S(2)}) copy-start(f32[3,768]{1,0:T(4,128)} %gains.1) | copy-start | bytes 27652
  0.6 9.8 %copy-start.1 = (f32[3,5,768]{2,0,1:T(4,128)S(1)}, f32[3,5,768]{2,0,1:T(4,128)}, u32[]{:S(2)}) copy-start(f32[3,5,768]{2,0,1:T(4,128)} %param.11) | copy-start | bytes 138244
  0.7 9.8 %copy-start.3 = (bf16[768,128]{1,0:T(8,128)(2,1)S(1)}, bf16[768,128]{1,0:T(8,128)(2,1)}, u32[]{:S(2)}) copy-start(bf16[768,128]{1,0:T(8,128)(2,1)} %key_w.1) | copy-start | bytes 589828
  0.7 9.8 %copy-start.2 = (bf16[768,128]{1,0:T(8,128)(2,1)S(1)}, bf16[768,128]{1,0:T(8,128)(2,1)}, u32[]{:S(2)}) copy-start(bf16[768,128]{1,0:T(8,128)(2,1)} %query_w.1) | copy-start | bytes 589828
  0.7 8.6 %collective-permute-start = (s32[256,128]{1,0:T(8,128)}, s32[256,128]{1,0:T(8,128)S(1)}, u32[]{:S(2)}, u32[]{:S(2)}) collective-permute-start(s32[256,128]{1,0:T(8,128)} %own_hbm.1), channel_id=1, source_target_pairs={{0,8},{8,0},{1,9},{9,1},{2,10},{10,2},{3,11},{11,3},{4,12},{12,4},... | collective-permute-start | bytes 393224 | tf_op jit(solution)/shard_map/ppermute | solution.py:257
  4.0 6.5 %collective-permute-start.1 = (s32[256,128]{1,0:T(8,128)}, s32[256,128]{1,0:T(8,128)S(1)}, u32[]{:S(2)}, u32[]{:S(2)}) collective-permute-start(s32[256,128]{1,0:T(8,128)} %own_hbm.1), channel_id=1, source_target_pairs={{8,16},{16,8},{24,32},{32,24},{40,48},{48,40},{56,64},{64,56},{72,... | collective-permute-start | bytes 393224 | tf_op jit(solution)/shard_map/ppermute | solution.py:258
  10.5 24.3 %copy-start = (bf16[3,3,128,128]{3,2,1,0:T(8,128)(2,1)S(1)}, bf16[3,3,128,128]{3,2,1,0:T(8,128)(2,1)}, u32[]{:S(2)}) copy-start(bf16[3,3,128,128]{3,2,1,0:T(8,128)(2,1)} %kernel.1) | copy-start | bytes 884740
  32.2 3.6 %collective-permute-start.2 = (bf16[16,16,128]{2,1,0:T(8,128)(2,1)S(1)}, bf16[16,16,128]{2,1,0:T(8,128)(2,1)S(1)}, u32[]{:S(2)}, u32[]{:S(2)}) collective-permute-start(bf16[16,16,128]{2,1,0:T(8,128)(2,1)S(1)} %all_to_all.5.own), channel_id=1, source_target_pairs={{0,8},{8,0},{1,9},{9,1},{2,10},{10,2},{3,11},{11,3},{4,12},{12,4},... | collective-permute-start | bytes 196616 | tf_op jit(solution)/shard_map/ppermute | solution.py:309

commit v5 on v4

--- a/solution.py
+++ b/solution.py
@@ -40,7 +40,7 @@
 
 
 def one_hot_rows(codes, spread):
-    repeated = jnp.dot(codes.astype(F32).astype(BF16), spread, preferred_element_type=F32)
+    repeated = jnp.dot(codes, spread, preferred_element_type=F32)
     base = (lax.broadcasted_iota(jnp.int32, repeated.shape, 1) % 4).astype(F32)
     return jnp.where(repeated == base, 1.0, 0.0).astype(BF16)
 
@@ -108,7 +108,7 @@
     copies[0].wait()
     for half in range(2):
         rows = slice(half * 128, half * 128 + 128)
-        a_ref[rows, 0 : 4 * BASES] = one_hot_rows(own[rows, :], spread)
+        a_ref[rows, 0 : 4 * BASES] = one_hot_rows(own[rows, :].astype(F32).astype(BF16), spread)
     copies[1].wait()
     x_ref[HALO : HALO + SLAB, :] = jnp.dot(
         a_ref[:, 0 : 4 * BASES], table[...], preferred_element_type=F32
@@ -134,8 +134,8 @@
     del x_in, n_in
     place = lax.axis_index(("x_hi", "z", "core"))
     core = lax.axis_index("core")
-    low_bases = jnp.where(core == 0, outer[SLAB - HALO :, :], inner[SLAB - HALO :, :])
-    high_bases = jnp.where(core == 0, inner[:HALO, :], outer[:HALO, :])
+    low_bases = jnp.where(core == 0, outer[...], inner[...])
+    high_bases = jnp.where(core == 0, inner[...], outer[...])
     spread = spread_matrix()
     a_ref[0:HALO, 0 : 4 * BASES] = one_hot_rows(low_bases, spread)
     a_ref[HALO : 2 * HALO, 0 : 4 * BASES] = one_hot_rows(high_bases, spread)
@@ -183,7 +183,9 @@
         keys_out[peer] = mine
 
 
-def weights_kernel(queries, kernel, weights, wide_q):
+def weights_kernel(queries, kernel, trunk, weights, trunk_hbm, wide_q, sem):
+    copy = pltpu.make_async_copy(trunk, trunk_hbm, sem)
+    copy.start()
     flipped = jnp.transpose(queries[...], (1, 0)) * 0.5
     for i in range(18):
         wide_q[i] = jnp.broadcast_to(flipped[:, i : i + 1], (PC, PC)).astype(BF16)
@@ -199,6 +201,7 @@
         return 0
 
     lax.fori_loop(0, 8, two_rows, 0)
+    copy.wait()
 
 
 def pair_kernel_body(queries, own, other, weights, out_hbm, key_cat, key_f, out_ref, sems):
@@ -250,12 +253,18 @@
 def on_device(
     bases, embed_table, norm_gains, depth_taps, point_weight, query_weight, key_weight, pair_kernel
 ):
+    core = lax.axis_index("core")
     seq = ("x_hi", "z", "core")
     outer_pairs = []
     for i in range(1, 31, 2):
         outer_pairs += [(i, i + 1), (i + 1, i)]
-    inner = lax.ppermute(bases, "core", [(0, 1), (1, 0)])
-    outer = lax.ppermute(bases, seq, outer_pairs)
+    toward_core = jnp.where(core == 0, SLAB - HALO, 0)
+    ends = [
+        lax.dynamic_slice(bases, (start, 0), (HALO, BASES)).astype(BF16)
+        for start in (toward_core, SLAB - HALO - toward_core)
+    ]
+    inner = lax.ppermute(ends[0], "core", [(0, 1), (1, 0)])
+    outer = lax.ppermute(ends[1], seq, outer_pairs)
 
     taps = jnp.transpose(depth_taps, (1, 0, 2))
     hbm_space = [pl.BlockSpec(memory_space=pltpu.HBM)]
@@ -308,18 +317,21 @@
     own_keys = lax.all_to_all(keys, ("x_hi", "z"), 0, 0, tiled=False)
     other_keys = lax.ppermute(own_keys, "core", [(0, 1), (1, 0)])
 
-    weights = pl.pallas_call(
+    weights, trunk = pl.pallas_call(
         weights_kernel,
-        out_shape=jax.ShapeDtypeStruct((8, 3 * PC, 2 * PC), BF16),
-        in_specs=vmem(2),
-        out_specs=vmem(1)[0],
-        scratch_shapes=[pltpu.VMEM((18, PC, PC), BF16)],
+        out_shape=(
+            jax.ShapeDtypeStruct((8, 3 * PC, 2 * PC), BF16),
+            jax.ShapeDtypeStruct((SLAB, C), BF16),
+        ),
+        in_specs=vmem(3),
+        out_specs=(vmem(1)[0], pl.BlockSpec(memory_space=pl.ANY)),
+        scratch_shapes=[pltpu.VMEM((18, PC, PC), BF16), pltpu.SemaphoreType.DMA],
         compiler_params=pltpu.CompilerParams(vmem_limit_bytes=8 * 1024 * 1024),
         cost_estimate=pl.CostEstimate(
             flops=400_000_000, bytes_accessed=2_000_000, transcendentals=0
         ),
         name="weights",
-    )(queries, pair_kernel)
+    )(queries, pair_kernel, trunk)
     pair_map = pl.pallas_call(
         pair_kernel_body,
         out_shape=jax.ShapeDtypeStruct((16, 512, PC), BF16),

time: 38.2 us -> 37.3 us (0.976)
  waiting for transfers between devices: 1.12 us -> 0.01 us
  other arithmetic: 0 us -> 0.93 us
  starting transfers between devices: 7.7 us -> 6.93 us
  Pallas kernels: 10.5 us -> 9.98 us
  blocking collectives: 18 us -> 18.5 us
    ppermute x2, waiting for transfers between devices: 1.12 us -> 0.01 us  [the longest x1 0.01 us: on_device(): outer = lax.ppermute(ends[1], seq, outer_pairs)]
    convert_element_type x0 -> x1, other arithmetic: none -> 0.93 us  [on_device(): lax.dynamic_slice(bases, (start, 0), (HALO, BASES)).astype(BF16)]
    ppermute x1, starting transfers between devices: 2.5 us -> 1.92 us  [on_device(): other_keys = lax.ppermute(own_keys, 'core', [(0, 1), (1, 0)])]
    pallas_call x1, Pallas kernels: 3.74 us -> 3.2 us  [on_device(): pl.pallas_call(outer_kernel, out_shape=(jax.ShapeDtypeStruct((SLAB, C), B...]
    all_to_all x1, blocking collectives: 18 us -> 18.5 us  [on_device(): own_keys = lax.all_to_all(keys, ('x_hi', 'z'), 0, 0, tiled=False)]
  transfers between devices with their start and end apart: 3 -> 3, of which waited for: 1 -> 0; matrix products, arithmetic and copies ran while one was open for 0% -> 0% of each run, Pallas kernels for 12% -> 12%
where the time goes in v5:
time: 37.3 us; the launch traced here: 37.2 us
  blocking collectives  18.5 us (50%)
  Pallas kernels  9.98 us (27%)
  starting transfers between devices  6.93 us (19%)
  other arithmetic  0.93 us (2%)
  between operations  0.78 us (2%)
    all_to_all x1, blocking collectives, on_device(): own_keys = lax.all_to_all(keys, ('x_hi', 'z'), 0, 0, tiled=False)  18.5 us
    ppermute x1, starting transfers between devices, on_device(): outer = lax.ppermute(ends[1], seq, outer_pairs)  4.92 us
    pallas_call x1, Pallas kernels, on_device(): pl.pallas_call(inner_kernel, out_shape=state + (jax.ShapeDtypeStruct((4 *...  3.5 us
    pallas_call x1, Pallas kernels, on_device(): pl.pallas_call(outer_kernel, out_shape=(jax.ShapeDtypeStruct((SLAB, C), B...  3.2 us
    pallas_call x1, Pallas kernels, on_device(): pl.pallas_call(pair_kernel_body, out_shape=jax.ShapeDtypeStruct((16, 512,...  2.15 us
    ppermute x1, starting transfers between devices, on_device(): other_keys = lax.ppermute(own_keys, 'core', [(0, 1), (1, 0)])  1.92 us
    pallas_call x1, Pallas kernels, on_device(): pl.pallas_call(weights_kernel, out_shape=(jax.ShapeDtypeStruct((8, 3 * PC...  1.13 us
    convert_element_type x1, other arithmetic, on_device(): lax.dynamic_slice(bases, (start, 0), (HALO, BASES)).astype(BF16)  0.93 us
  transfers between devices with their start and end apart: 3, of which 0 were waited for; matrix products, arithmetic and copies ran while one was open for 0% of the time, Pallas kernels for 12%

profile of v5, /device:TPU:1, one launch (start us, length us, event | category | flops | bytes accessed | tf_op | source)
XLA Modules:
  0.0 37.2 jit_solution(16808805831791102408)
XLA Ops:
  0.6 0.0 copy-start.3
  0.6 0.0 copy-start
  0.7 0.0 copy-start.2
  0.7 0.0 copy-start.1
  0.7 0.9 %dynamic-slice_convert_fusion = (bf16[112,128]{1,0:T(8,128)(2,1)S(1)}, bf16[112,128]{1,0:T(8,128)(2,1)S(1)}) fusion(s32[256,128]{1,0:T(8,128)} %own_hbm.1, s32[]{:T(128)S(6)} %select_n.9, s32[]{:T(128)S(6)} %select_n.8), kind=kLoop, calls=%fused_computation | loop fusion | flops 28672 | bytes 172040 | tf_op jit(solution)/shard_map/convert_element_type | solution.py:263
  1.6 4.9 %collective-permute-start.1 = (bf16[112,128]{1,0:T(8,128)(2,1)S(1)}, bf16[112,128]{1,0:T(8,128)(2,1)S(1)}, u32[]{:S(2)}, u32[]{:S(2)}) collective-permute-start(bf16[112,128]{1,0:T(8,128)(2,1)S(1)} %get-tuple-element.20), channel_id=1, source_target_pairs={{8,16},{16,8},{24,32},{32,24},{40,48},{48,40},{56,64},{64,56},{72,... | collective-permute-start | bytes 86024 | tf_op jit(solution)/shard_map/ppermute | solution.py:267
  6.5 0.1 collective-permute-start
  6.6 3.5 %inner.1 = (f32[480,768]{1,0:T(8,128)S(1)}, f32[3,6,480,128]{3,2,1,0:T(8,128)S(1)}, bf16[512,768]{1,0:T(8,128)(2,1)S(1)}, bf16[3,768,768]{2,1,0:T(8,128)(2,1)S(1)}) custom-call(s32[256,128]{1,0:T(8,128)} %own_hbm.1, bf16[512,768]{1,0:T(8,128)(2,1)} %table_hbm.1, f32[3,768]{1,0:T(4,128)} %gains.1, f32[5,3,768]{2,1,0:T(4,128)} %bitcast.1, ...), custom_call_target="tpu_custom_call" | custom-call | flops 800000000 | bytes 5000000 | tf_op jit(solution)/shard_map/inner/pallas_call | solution.py:275
  10.2 0.0 collective-permute-done.1.outer
  10.2 0.0 collective-permute-done.inner
  10.2 0.0 copy-done.3
  10.2 0.0 copy-done
  10.2 0.0 copy-done.2
  10.2 0.0 copy-done.1
  10.2 0.0 copy-start.4
  10.2 3.2 %outer.1 = (bf16[256,768]{1,0:T(8,128)(2,1)S(1)}, bf16[16,16,128]{2,1,0:T(8,128)(2,1)S(1)}, f32[32,128]{1,0:T(8,128)S(1)}, f32[480,768]{1,0:T(8,128)S(1)}, f32[3,6,480,128]{3,2,1,0:T(8,128)S(1)}) custom-call(bf16[112,128]{1,0:T(8,128)(2,1)S(1)} %collective-permute-done.inner, ...), custom_call_target="tpu_custom_call", output_to_operand_aliasing={{3}: (8, {}), {4}: (9, {})} | custom-call | flops 1000000000 | bytes 1000000 | tf_op jit(solution)/shard_map/outer/pallas_call | solution.py:298
  13.4 18.5 %all_to_all.5.own = bf16[16,16,128]{2,1,0:T(8,128)(2,1)S(1)} all-to-all(bf16[16,16,128]{2,1,0:T(8,128)(2,1)S(1)} %get-tuple-element.18), channel_id=1, replica_groups=mesh['x_hi'=2,'z'=8,'core'=2,'batch'=8] {'x_hi','z'}, dimensions={0} | all-to-all | bytes 131072 | tf_op jit(solution)/shard_map/all_to_all | solution.py:317
  32.0 1.9 %collective-permute-start.2 = (bf16[16,16,128]{2,1,0:T(8,128)(2,1)S(1)}, bf16[16,16,128]{2,1,0:T(8,128)(2,1)S(1)}, u32[]{:S(2)}, u32[]{:S(2)}) collective-permute-start(bf16[16,16,128]{2,1,0:T(8,128)(2,1)S(1)} %all_to_all.5.own), channel_id=1, source_target_pairs={{0,8},{8,0},{1,9},{9,1},{2,10},{10,2},{3,11},{11,3},{4,12},{12,4},... | collective-permute-start | bytes 196616 | tf_op jit(solution)/shard_map/ppermute | solution.py:318
  33.9 0.0 copy-done.4
  33.9 1.1 %weights.1 = (bf16[8,384,256]{2,1,0:T(8,128)(2,1)S(1)}, bf16[256,768]{1,0:T(8,128)(2,1)}) custom-call(f32[32,128]{1,0:T(8,128)S(1)} %get-tuple-element.15.queries, bf16[3,3,128,128]{3,2,1,0:T(8,128)(2,1)S(1)} %copy-done.4, bf16[256,768]{1,0:T(8,128)(2,1)S(1)} %get-tuple-element.16.trunk), custom_call_target="tpu_custom_call" | custom-call | flops 400000000 | bytes 2000000 | tf_op jit(solution)/shard_map/weights/pallas_call | solution.py:320
  35.0 0.0 collective-permute-done.2.other
  35.0 2.1 %pair.1 = bf16[16,512,128]{2,1,0:T(8,128)(2,1)} custom-call(f32[32,128]{1,0:T(8,128)S(1)} %get-tuple-element.15.queries, bf16[16,16,128]{2,1,0:T(8,128)(2,1)S(1)} %all_to_all.5.own, bf16[16,16,128]{2,1,0:T(8,128)(2,1)S(1)} %collective-permute-done.2.other, bf16[8,384,256]{2,1,0:T(8,128)(2,1)S(1)} %get-tuple-element.19.weights), custom_call_target="tpu_custom_call" | custom-call | tf_op jit(solution)/shard_map/pair/pallas_call | solution.py:335
Async XLA Ops:
  0.6 9.6 %copy-start.3 = (f32[3,768]{1,0:T(4,128)S(1)}, f32[3,768]{1,0:T(4,128)}, u32[]{:S(2)}) copy-start(f32[3,768]{1,0:T(4,128)} %gains.1) | copy-start | bytes 27652
  0.6 9.5 %copy-start = (f32[3,5,768]{2,0,1:T(4,128)S(1)}, f32[3,5,768]{2,0,1:T(4,128)}, u32[]{:S(2)}) copy-start(f32[3,5,768]{2,0,1:T(4,128)} %param.11) | copy-start | bytes 138244
  0.7 9.5 %copy-start.2 = (bf16[768,128]{1,0:T(8,128)(2,1)S(1)}, bf16[768,128]{1,0:T(8,128)(2,1)}, u32[]{:S(2)}) copy-start(bf16[768,128]{1,0:T(8,128)(2,1)} %key_w.1) | copy-start | bytes 589828
  0.7 9.5 %copy-start.1 = (bf16[768,128]{1,0:T(8,128)(2,1)S(1)}, bf16[768,128]{1,0:T(8,128)(2,1)}, u32[]{:S(2)}) copy-start(bf16[768,128]{1,0:T(8,128)(2,1)} %query_w.1) | copy-start | bytes 589828
  1.6 8.5 %collective-permute-start.1 = (bf16[112,128]{1,0:T(8,128)(2,1)S(1)}, bf16[112,128]{1,0:T(8,128)(2,1)S(1)}, u32[]{:S(2)}, u32[]{:S(2)}) collective-permute-start(bf16[112,128]{1,0:T(8,128)(2,1)S(1)} %get-tuple-element.20), channel_id=1, source_target_pairs={{8,16},{16,8},{24,32},{32,24},{40,48},{48,40},{56,64},{64,56},{72,... | collective-permute-start | bytes 86024 | tf_op jit(solution)/shard_map/ppermute | solution.py:267
  6.5 3.6 %collective-permute-start = (bf16[112,128]{1,0:T(8,128)(2,1)S(1)}, bf16[112,128]{1,0:T(8,128)(2,1)S(1)}, u32[]{:S(2)}, u32[]{:S(2)}) collective-permute-start(bf16[112,128]{1,0:T(8,128)(2,1)S(1)} %get-tuple-element.21), channel_id=1, source_target_pairs={{0,8},{8,0},{1,9},{9,1},{2,10},{10,2},{3,11},{11,3},{4,12},{12,4},... | collective-permute-start | bytes 86024 | tf_op jit(solution)/shard_map/ppermute | solution.py:266
  10.2 23.7 %copy-start.4 = (bf16[3,3,128,128]{3,2,1,0:T(8,128)(2,1)S(1)}, bf16[3,3,128,128]{3,2,1,0:T(8,128)(2,1)}, u32[]{:S(2)}) copy-start(bf16[3,3,128,128]{3,2,1,0:T(8,128)(2,1)} %kernel.1) | copy-start | bytes 884740
  32.0 3.1 %collective-permute-start.2 = (bf16[16,16,128]{2,1,0:T(8,128)(2,1)S(1)}, bf16[16,16,128]{2,1,0:T(8,128)(2,1)S(1)}, u32[]{:S(2)}, u32[]{:S(2)}) collective-permute-start(bf16[16,16,128]{2,1,0:T(8,128)(2,1)S(1)} %all_to_all.5.own), channel_id=1, source_target_pairs={{0,8},{8,0},{1,9},{9,1},{2,10},{10,2},{3,11},{11,3},{4,12},{12,4},... | collective-permute-start | bytes 196616 | tf_op jit(solution)/shard_map/ppermute | solution.py:318

commit v6 on v5

--- a/solution.py
+++ b/solution.py
@@ -91,44 +91,35 @@
         x_ref[start:stop, cols] = x_ref[start:stop, cols] + update
 
 
-def inner_kernel(
-    own_hbm, table_hbm, gains_hbm, taps_hbm, point_hbm,
-    x_ref, n_ref, table, point,
-    own, gains, taps, wide_taps, a_ref, sems,
-):
-    moves = [(own_hbm, own), (table_hbm, table), (gains_hbm, gains), (taps_hbm, taps)]
-    moves += [(point_hbm.at[layer], point.at[layer]) for layer in range(3)]
-    copies = [
-        pltpu.make_async_copy(source, target, sems.at[k])
-        for k, (source, target) in enumerate(moves)
-    ]
-    for copy in copies:
-        copy.start()
-    spread = spread_matrix()
-    copies[0].wait()
-    for half in range(2):
-        rows = slice(half * 128, half * 128 + 128)
-        a_ref[rows, 0 : 4 * BASES] = one_hot_rows(own[rows, :].astype(F32).astype(BF16), spread)
-    copies[1].wait()
-    x_ref[HALO : HALO + SLAB, :] = jnp.dot(
-        a_ref[:, 0 : 4 * BASES], table[...], preferred_element_type=F32
-    )
-    copies[2].wait()
-    copies[3].wait()
+def ends_kernel(bases_hbm, to_core, to_chip, codes, spread, own, sem):
+    copy = pltpu.make_async_copy(bases_hbm, own, sem)
+    copy.start()
+    spread[...] = spread_matrix()
+    core = lax.axis_index("core")
+    copy.wait()
+    rows = own[...].astype(F32)
+    head = rows[:HALO].astype(BF16)
+    tail = rows[SLAB - HALO :].astype(BF16)
+    to_core[...] = jnp.where(core == 0, tail, head)
+    to_chip[...] = jnp.where(core == 0, head, tail)
+    codes[...] = rows.astype(BF16)
+
+
+def inner_kernel(codes, spread, table, gains, taps, point, x_ref, n_ref, wide_taps, a_ref):
+    one_hot = one_hot_rows(codes[...], spread[...])
+    x_ref[HALO : HALO + SLAB, :] = jnp.dot(one_hot, table[...], preferred_element_type=F32)
     spread_taps(taps, gains, wide_taps)
     norm_rows(x_ref, n_ref, 0, 112, 368)
     for layer, low, high in ((0, 128, 352), (1, 144, 336)):
-        copies[4 + layer].wait()
         middle = (low + high) // 2
         for start, stop in ((low, middle), (middle, high)):
             conv_rows(n_ref, a_ref, layer, wide_taps, start, stop, start - low)
             mix(a_ref, x_ref, point.at[layer], start, stop, start - low)
             norm_rows(x_ref, n_ref, layer + 1, start, stop)
-    copies[6].wait()
 
 
 def outer_kernel(
-    inner, outer, gains, taps, table, point, query_w, key_w, x_in, n_in,
+    inner, outer, spread, gains, taps, table, point, query_w, key_w, x_in, n_in,
     trunk_out, keys_out, query_out, x_ref, n_ref, wide_taps, a_ref,
 ):
     del x_in, n_in
@@ -136,9 +127,8 @@
     core = lax.axis_index("core")
     low_bases = jnp.where(core == 0, outer[...], inner[...])
     high_bases = jnp.where(core == 0, inner[...], outer[...])
-    spread = spread_matrix()
-    a_ref[0:HALO, 0 : 4 * BASES] = one_hot_rows(low_bases, spread)
-    a_ref[HALO : 2 * HALO, 0 : 4 * BASES] = one_hot_rows(high_bases, spread)
+    a_ref[0:HALO, 0 : 4 * BASES] = one_hot_rows(low_bases, spread[...])
+    a_ref[HALO : 2 * HALO, 0 : 4 * BASES] = one_hot_rows(high_bases, spread[...])
     x_ref[0:HALO, :] = jnp.dot(
         a_ref[0:HALO, 0 : 4 * BASES], table[...], preferred_element_type=F32
     )
@@ -253,48 +243,47 @@
 def on_device(
     bases, embed_table, norm_gains, depth_taps, point_weight, query_weight, key_weight, pair_kernel
 ):
-    core = lax.axis_index("core")
     seq = ("x_hi", "z", "core")
     outer_pairs = []
     for i in range(1, 31, 2):
         outer_pairs += [(i, i + 1), (i + 1, i)]
-    toward_core = jnp.where(core == 0, SLAB - HALO, 0)
-    ends = [
-        lax.dynamic_slice(bases, (start, 0), (HALO, BASES)).astype(BF16)
-        for start in (toward_core, SLAB - HALO - toward_core)
-    ]
-    inner = lax.ppermute(ends[0], "core", [(0, 1), (1, 0)])
-    outer = lax.ppermute(ends[1], seq, outer_pairs)
+    to_core, to_chip, codes, spread = pl.pallas_call(
+        ends_kernel,
+        out_shape=(
+            jax.ShapeDtypeStruct((HALO, BASES), BF16),
+            jax.ShapeDtypeStruct((HALO, BASES), BF16),
+            jax.ShapeDtypeStruct((SLAB, BASES), BF16),
+            jax.ShapeDtypeStruct((BASES, 4 * BASES), BF16),
+        ),
+        in_specs=[pl.BlockSpec(memory_space=pltpu.HBM)],
+        out_specs=tuple(vmem(4)),
+        scratch_shapes=[pltpu.VMEM((SLAB, BASES), jnp.int32), pltpu.SemaphoreType.DMA],
+        compiler_params=pltpu.CompilerParams(vmem_limit_bytes=4 * 1024 * 1024),
+        cost_estimate=pl.CostEstimate(
+            flops=20_000_000_000, bytes_accessed=1_000_000, transcendentals=0
+        ),
+        name="ends",
+    )(in_hbm(bases))
+    inner = lax.ppermute(to_core, "core", [(0, 1), (1, 0)])
+    outer = lax.ppermute(to_chip, seq, outer_pairs)
 
     taps = jnp.transpose(depth_taps, (1, 0, 2))
-    hbm_space = [pl.BlockSpec(memory_space=pltpu.HBM)]
     state = (
         jax.ShapeDtypeStruct((ROWS, C), F32),
         jax.ShapeDtypeStruct((3, C // 128, ROWS, 128), F32),
     )
-    x, n, table, point = pl.pallas_call(
+    x, n = pl.pallas_call(
         inner_kernel,
-        out_shape=state
-        + (
-            jax.ShapeDtypeStruct((4 * BASES, C), BF16),
-            jax.ShapeDtypeStruct((3, C, C), BF16),
-        ),
-        in_specs=hbm_space * 5,
-        out_specs=tuple(vmem(4)),
-        scratch_shapes=[
-            pltpu.VMEM((SLAB, BASES), jnp.int32),
-            pltpu.VMEM((3, C), F32),
-            pltpu.VMEM((5, 3, C), F32),
-            pltpu.VMEM((3, 5, 8, C), F32),
-            pltpu.VMEM((SLAB, C), BF16),
-            pltpu.SemaphoreType.DMA((7,)),
-        ],
-        compiler_params=pltpu.CompilerParams(vmem_limit_bytes=16 * 1024 * 1024),
+        out_shape=state,
+        in_specs=vmem(6),
+        out_specs=tuple(vmem(2)),
+        scratch_shapes=[pltpu.VMEM((3, 5, 8, C), F32), pltpu.VMEM((SLAB, C), BF16)],
+        compiler_params=pltpu.CompilerParams(vmem_limit_bytes=12 * 1024 * 1024),
         cost_estimate=pl.CostEstimate(
             flops=800_000_000, bytes_accessed=5_000_000, transcendentals=400_000
         ),
         name="inner",
-    )(in_hbm(bases), in_hbm(embed_table), in_hbm(norm_gains), in_hbm(taps), in_hbm(point_weight))
+    )(codes, spread, embed_table, norm_gains, taps, point_weight)
     trunk, keys, queries, _, _ = pl.pallas_call(
         outer_kernel,
         out_shape=(
@@ -303,16 +292,18 @@
             jax.ShapeDtypeStruct((32, PC), F32),
         )
         + state,
-        in_specs=vmem(10),
+        in_specs=vmem(11),
         out_specs=tuple(vmem(5)),
         scratch_shapes=[pltpu.VMEM((3, 5, 8, C), F32), pltpu.VMEM((288, C), BF16)],
-        input_output_aliases={8: 3, 9: 4},
+        input_output_aliases={9: 3, 10: 4},
         compiler_params=pltpu.CompilerParams(vmem_limit_bytes=16 * 1024 * 1024),
         cost_estimate=pl.CostEstimate(
             flops=1_000_000_000, bytes_accessed=1_000_000, transcendentals=600_000
         ),
         name="outer",
-    )(inner, outer, norm_gains, taps, table, point, query_weight, key_weight, x, n)
+    )(
+        inner, outer, spread, norm_gains, taps, embed_table, point_weight, query_weight, key_weight, x, n
+    )
 
     own_keys = lax.all_to_all(keys, ("x_hi", "z"), 0, 0, tiled=False)
     other_keys = lax.ppermute(own_keys, "core", [(0, 1), (1, 0)])

time: 37.3 us -> 37.4 us (level)
  starting transfers between devices: 6.93 us -> 8.01 us
  waiting for transfers between devices: 0.01 us -> 1 us
  other arithmetic: 0.93 us -> 0 us
  blocking collectives: 18.5 us -> 17.7 us
    ppermute x2, waiting for transfers between devices: 0.01 us -> 1 us  [the longest x1 0.99 us: on_device(): outer = lax.ppermute(to_chip, seq, outer_pairs)]
    convert_element_type x1 -> x0, other arithmetic: 0.93 us -> none  [on_device(): lax.dynamic_slice(bases, (start, 0), (HALO, BASES)).astype(BF16)]
    ppermute x1, starting transfers between devices: 1.92 us -> 2.81 us  [on_device(): other_keys = lax.ppermute(own_keys, 'core', [(0, 1), (1, 0)])]
    all_to_all x1, blocking collectives: 18.5 us -> 17.7 us  [on_device(): own_keys = lax.all_to_all(keys, ('x_hi', 'z'), 0, 0, tiled=False)]
    pallas_call x1 -> x2, Pallas kernels: 3.5 us -> 3.26 us  [the longest x1 2.18 us: on_device(): pl.pallas_call(inner_kernel, out_shape=state, in_specs=vmem(6), out_specs...]
  transfers between devices with their start and end apart: 3 -> 3, of which waited for: 0 -> 1; matrix products, arithmetic and copies ran while one was open for 0% -> 0% of each run, Pallas kernels for 12% -> 9%
where the time goes in v6:
time: 37.4 us; the launch traced here: 37.3 us
  blocking collectives  17.7 us (47%)
  Pallas kernels  9.75 us (26%)
  starting transfers between devices  8.01 us (21%)
  waiting for transfers between devices  1 us (3%)
  between operations  0.77 us (2%)
    all_to_all x1, blocking collectives, on_device(): own_keys = lax.all_to_all(keys, ('x_hi', 'z'), 0, 0, tiled=False)  17.7 us
    ppermute x1, starting transfers between devices, on_device(): inner = lax.ppermute(to_core, 'core', [(0, 1), (1, 0)])  3.29 us
    pallas_call x1, Pallas kernels, on_device(): pl.pallas_call(outer_kernel, out_shape=(jax.ShapeDtypeStruct((SLAB, C), B...  3.21 us
    ppermute x1, starting transfers between devices, on_device(): other_keys = lax.ppermute(own_keys, 'core', [(0, 1), (1, 0)])  2.81 us
    pallas_call x1, Pallas kernels, on_device(): pl.pallas_call(inner_kernel, out_shape=state, in_specs=vmem(6), out_specs...  2.18 us
    pallas_call x1, Pallas kernels, on_device(): pl.pallas_call(pair_kernel_body, out_shape=jax.ShapeDtypeStruct((16, 512,...  2.14 us
    ppermute x1, starting transfers between devices, on_device(): outer = lax.ppermute(to_chip, seq, outer_pairs)  1.91 us
    pallas_call x1, Pallas kernels, on_device(): pl.pallas_call(weights_kernel, out_shape=(jax.ShapeDtypeStruct((8, 3 * PC...  1.13 us
  transfers between devices with their start and end apart: 3, of which 1 were waited for; matrix products, arithmetic and copies ran while one was open for 0% of the time, Pallas kernels for 9%

profile of v6, /device:TPU:1, one launch (start us, length us, event | category | flops | bytes accessed | tf_op | source)
XLA Modules:
  0.0 37.3 jit_solution(3722984626615369156)
XLA Ops:
  0.6 0.0 copy-start
  0.6 0.0 copy-start.5
  0.7 0.0 copy-start.1
  0.7 0.0 copy-start.2
  0.7 1.1 %ends.1 = (bf16[112,128]{1,0:T(8,128)(2,1)S(1)}, bf16[112,128]{1,0:T(8,128)(2,1)S(1)}, bf16[256,128]{1,0:T(8,128)(2,1)S(1)}, bf16[128,512]{1,0:T(8,128)(2,1)S(1)}) custom-call(s32[256,128]{1,0:T(8,128)} %bases_hbm.1), custom_call_target="tpu_custom_call" | custom-call | flops 20000000000 | bytes 1000000 | tf_op jit(solution)/shard_map/ends/pallas_call | solution.py:250
  1.8 3.3 %collective-permute-start = (bf16[112,128]{1,0:T(8,128)(2,1)S(1)}, bf16[112,128]{1,0:T(8,128)(2,1)S(1)}, u32[]{:S(2)}, u32[]{:S(2)}) collective-permute-start(bf16[112,128]{1,0:T(8,128)(2,1)S(1)} %get-tuple-element.13), channel_id=1, source_target_pairs={{0,8},{8,0},{1,9},{9,1},{2,10},{10,2},{3,11},{11,3},{4,12},{12,4},... | collective-permute-start | bytes 86024 | tf_op jit(solution)/shard_map/ppermute | solution.py:267
  5.0 1.9 %collective-permute-start.1 = (bf16[112,128]{1,0:T(8,128)(2,1)S(1)}, bf16[112,128]{1,0:T(8,128)(2,1)S(1)}, u32[]{:S(2)}, u32[]{:S(2)}) collective-permute-start(bf16[112,128]{1,0:T(8,128)(2,1)S(1)} %get-tuple-element.14), channel_id=1, source_target_pairs={{8,16},{16,8},{24,32},{32,24},{40,48},{48,40},{56,64},{64,56},{72,... | collective-permute-start | bytes 86024 | tf_op jit(solution)/shard_map/ppermute | solution.py:268
  7.0 0.0 copy-done
  7.0 0.0 copy-done.5
  7.0 0.0 copy-done.1
  7.0 0.0 copy-done.2
  7.0 0.0 copy-start.3
  7.0 0.0 copy-start.4
  7.0 2.2 %inner.1 = (f32[480,768]{1,0:T(8,128)S(1)}, f32[3,6,480,128]{3,2,1,0:T(8,128)S(1)}) custom-call(bf16[256,128]{1,0:T(8,128)(2,1)S(1)} %get-tuple-element.16.codes, bf16[128,512]{1,0:T(8,128)(2,1)S(1)} %get-tuple-element.15.spread, bf16[512,768]{1,0:T(8,128)(2,1)S(1)} %copy-done.1, f32[3,768]{1,0:T(4,128)S(1)} %copy-done.5, f32[5,3,768]{2,1,0:T(4,128)S(1)} %bitcast.1, ...), custom_call_target="tpu_custom_call" | custom-call | flops 800000000 | bytes 5000000 | tf_op jit(solution)/shard_map/inner/pallas_call | solution.py:275
  9.2 0.0 collective-permute-done.inner
  9.2 1.0 %collective-permute-done.1.outer = bf16[112,128]{1,0:T(8,128)(2,1)S(1)} collective-permute-done((bf16[112,128]{1,0:T(8,128)(2,1)S(1)}, bf16[112,128]{1,0:T(8,128)(2,1)S(1)}, u32[]{:S(2)}, u32[]{:S(2)}) %collective-permute-start.1) | collective-permute-done | bytes 28704 | tf_op jit(solution)/shard_map/ppermute | solution.py:268
  10.2 0.0 copy-done.3
  10.2 0.0 copy-done.4
  10.2 0.0 copy-start.6
  10.2 3.2 %outer.1 = (bf16[256,768]{1,0:T(8,128)(2,1)S(1)}, bf16[16,16,128]{2,1,0:T(8,128)(2,1)S(1)}, f32[32,128]{1,0:T(8,128)S(1)}, f32[480,768]{1,0:T(8,128)S(1)}, f32[3,6,480,128]{3,2,1,0:T(8,128)S(1)}) custom-call(bf16[112,128]{1,0:T(8,128)(2,1)S(1)} %collective-permute-done.inner, ...), custom_call_target="tpu_custom_call", output_to_operand_aliasing={{3}: (9, {}), {4}: (10, {})} | custom-call | flops 1000000000 | bytes 1000000 | tf_op jit(solution)/shard_map/outer/pallas_call | solution.py:287
  13.4 17.7 %all_to_all.5.own = bf16[16,16,128]{2,1,0:T(8,128)(2,1)S(1)} all-to-all(bf16[16,16,128]{2,1,0:T(8,128)(2,1)S(1)} %get-tuple-element.22), channel_id=1, replica_groups=mesh['x_hi'=2,'z'=8,'core'=2,'batch'=8] {'x_hi','z'}, dimensions={0} | all-to-all | bytes 131072 | tf_op jit(solution)/shard_map/all_to_all | solution.py:308
  31.2 2.8 %collective-permute-start.2 = (bf16[16,16,128]{2,1,0:T(8,128)(2,1)S(1)}, bf16[16,16,128]{2,1,0:T(8,128)(2,1)S(1)}, u32[]{:S(2)}, u32[]{:S(2)}) collective-permute-start(bf16[16,16,128]{2,1,0:T(8,128)(2,1)S(1)} %all_to_all.5.own), channel_id=1, source_target_pairs={{0,8},{8,0},{1,9},{9,1},{2,10},{10,2},{3,11},{11,3},{4,12},{12,4},... | collective-permute-start | bytes 196616 | tf_op jit(solution)/shard_map/ppermute | solution.py:309
  34.0 0.0 copy-done.6
  34.0 1.1 %weights.1 = (bf16[8,384,256]{2,1,0:T(8,128)(2,1)S(1)}, bf16[256,768]{1,0:T(8,128)(2,1)}) custom-call(f32[32,128]{1,0:T(8,128)S(1)} %get-tuple-element.19.queries, bf16[3,3,128,128]{3,2,1,0:T(8,128)(2,1)S(1)} %copy-done.6, bf16[256,768]{1,0:T(8,128)(2,1)S(1)} %get-tuple-element.20.trunk), custom_call_target="tpu_custom_call" | custom-call | flops 400000000 | bytes 2000000 | tf_op jit(solution)/shard_map/weights/pallas_call | solution.py:311
  35.1 0.0 collective-permute-done.2.other
  35.1 2.1 %pair.1 = bf16[16,512,128]{2,1,0:T(8,128)(2,1)} custom-call(f32[32,128]{1,0:T(8,128)S(1)} %get-tuple-element.19.queries, bf16[16,16,128]{2,1,0:T(8,128)(2,1)S(1)} %all_to_all.5.own, bf16[16,16,128]{2,1,0:T(8,128)(2,1)S(1)} %collective-permute-done.2.other, bf16[8,384,256]{2,1,0:T(8,128)(2,1)S(1)} %get-tuple-element.23.weights), custom_call_target="tpu_custom_call" | custom-call | tf_op jit(solution)/shard_map/pair/pallas_call | solution.py:326
Async XLA Ops:
  0.6 6.3 %copy-start = (bf16[3,768,768]{2,1,0:T(8,128)(2,1)S(1)}, bf16[3,768,768]{2,1,0:T(8,128)(2,1)}, u32[]{:S(2)}) copy-start(bf16[3,768,768]{2,1,0:T(8,128)(2,1)} %point.3) | copy-start | bytes 10616836
  0.6 6.3 %copy-start.5 = (f32[3,768]{1,0:T(4,128)S(1)}, f32[3,768]{1,0:T(4,128)}, u32[]{:S(2)}) copy-start(f32[3,768]{1,0:T(4,128)} %gains.3) | copy-start | bytes 27652
  0.7 6.3 %copy-start.1 = (bf16[512,768]{1,0:T(8,128)(2,1)S(1)}, bf16[512,768]{1,0:T(8,128)(2,1)}, u32[]{:S(2)}) copy-start(bf16[512,768]{1,0:T(8,128)(2,1)} %table.3) | copy-start | bytes 2359300
  0.7 6.3 %copy-start.2 = (f32[3,5,768]{2,0,1:T(4,128)S(1)}, f32[3,5,768]{2,0,1:T(4,128)}, u32[]{:S(2)}) copy-start(f32[3,5,768]{2,0,1:T(4,128)} %param.11) | copy-start | bytes 138244
  1.8 7.5 %collective-permute-start = (bf16[112,128]{1,0:T(8,128)(2,1)S(1)}, bf16[112,128]{1,0:T(8,128)(2,1)S(1)}, u32[]{:S(2)}, u32[]{:S(2)}) collective-permute-start(bf16[112,128]{1,0:T(8,128)(2,1)S(1)} %get-tuple-element.13), channel_id=1, source_target_pairs={{0,8},{8,0},{1,9},{9,1},{2,10},{10,2},{3,11},{11,3},{4,12},{12,4},... | collective-permute-start | bytes 86024 | tf_op jit(solution)/shard_map/ppermute | solution.py:267
  5.0 5.2 %collective-permute-start.1 = (bf16[112,128]{1,0:T(8,128)(2,1)S(1)}, bf16[112,128]{1,0:T(8,128)(2,1)S(1)}, u32[]{:S(2)}, u32[]{:S(2)}) collective-permute-start(bf16[112,128]{1,0:T(8,128)(2,1)S(1)} %get-tuple-element.14), channel_id=1, source_target_pairs={{8,16},{16,8},{24,32},{32,24},{40,48},{48,40},{56,64},{64,56},{72,... | collective-permute-start | bytes 86024 | tf_op jit(solution)/shard_map/ppermute | solution.py:268
  7.0 3.2 %copy-start.3 = (bf16[768,128]{1,0:T(8,128)(2,1)S(1)}, bf16[768,128]{1,0:T(8,128)(2,1)}, u32[]{:S(2)}) copy-start(bf16[768,128]{1,0:T(8,128)(2,1)} %query_w.1) | copy-start | bytes 589828
  7.0 3.2 %copy-start.4 = (bf16[768,128]{1,0:T(8,128)(2,1)S(1)}, bf16[768,128]{1,0:T(8,128)(2,1)}, u32[]{:S(2)}) copy-start(bf16[768,128]{1,0:T(8,128)(2,1)} %key_w.1) | copy-start | bytes 589828
  10.2 23.8 %copy-start.6 = (bf16[3,3,128,128]{3,2,1,0:T(8,128)(2,1)S(1)}, bf16[3,3,128,128]{3,2,1,0:T(8,128)(2,1)}, u32[]{:S(2)}) copy-start(bf16[3,3,128,128]{3,2,1,0:T(8,128)(2,1)} %kernel.1) | copy-start | bytes 884740
  31.2 4.0 %collective-permute-start.2 = (bf16[16,16,128]{2,1,0:T(8,128)(2,1)S(1)}, bf16[16,16,128]{2,1,0:T(8,128)(2,1)S(1)}, u32[]{:S(2)}, u32[]{:S(2)}) collective-permute-start(bf16[16,16,128]{2,1,0:T(8,128)(2,1)S(1)} %all_to_all.5.own), channel_id=1, source_target_pairs={{0,8},{8,0},{1,9},{9,1},{2,10},{10,2},{3,11},{11,3},{4,12},{12,4},... | collective-permute-start | bytes 196616 | tf_op jit(solution)/shard_map/ppermute | solution.py:309

commit v7 on v6

--- a/solution.py
+++ b/solution.py
@@ -45,16 +45,21 @@
     return jnp.where(repeated == base, 1.0, 0.0).astype(BF16)
 
 
-def norm_rows(x_ref, n_ref, layer, start, stop, scale=None):
-    for at in range(start, stop, STEP):
-        rows = x_ref[at : at + STEP, :]
+def rows_at(base, offset, count):
+    return pl.ds(base + offset, count)
+
+
+def norm_rows(x_ref, n_ref, layer, base, count, scales=None):
+    for k in range(count // STEP):
+        at = rows_at(base, k * STEP, STEP)
+        rows = x_ref[at, :]
         mean = jnp.sum(rows * rows, axis=-1, keepdims=True) * (1.0 / C)
         factor = lax.rsqrt(mean + 1e-06)
-        if scale is not None:
-            factor = factor * scale
+        if scales is not None and scales[k] is not None:
+            factor = factor * scales[k]
         rows = rows * factor
         for c in range(C // 128):
-            n_ref[layer, c, at : at + STEP, :] = rows[:, c * 128 : (c + 1) * 128]
+            n_ref[layer, c, at, :] = rows[:, c * 128 : (c + 1) * 128]
 
 
 def spread_taps(taps, gains, wide_taps):
@@ -65,30 +70,29 @@
             wide_taps[layer, t] = jnp.broadcast_to(row, (8, C))
 
 
-def conv_rows(n_ref, a_ref, layer, wide_taps, start, stop, to):
+def conv_rows(n_ref, a_ref, layer, wide_taps, base, count, to):
     reach = DILATIONS[layer]
-    for at in range(start, stop, STEP):
+    for k in range(0, count, STEP):
         for c in range(C // 128):
             cols = slice(c * 128, (c + 1) * 128)
             halves = []
-            for row in (at, at + 8):
+            for row in (k, k + 8):
                 half = None
                 for t in range(5):
-                    low = row + (t - 2) * reach
-                    term = n_ref[layer, c, low : low + 8, :] * wide_taps[layer, t, :, cols]
+                    piece = n_ref[layer, c, rows_at(base, row + (t - 2) * reach, 8), :]
+                    term = piece * wide_taps[layer, t, :, cols]
                     half = term if half is None else half + term
                 halves.append(half)
             half = jnp.concatenate(halves, axis=0)
-            a_ref[to + at - start : to + at - start + STEP, cols] = gelu_of_half(half)
-
-
-def mix(a_ref, x_ref, weights, start, stop, at):
+            a_ref[to + k : to + k + STEP, cols] = gelu_of_half(half)
+
+
+def mix(a_ref, x_ref, weights, base, count, to):
+    at = rows_at(base, 0, count)
     for strip in range(3):
         cols = slice(strip * 256, strip * 256 + 256)
-        update = jnp.dot(
-            a_ref[at : at + stop - start, :], weights[:, cols], preferred_element_type=F32
-        )
-        x_ref[start:stop, cols] = x_ref[start:stop, cols] + update
+        update = jnp.dot(a_ref[to : to + count, :], weights[:, cols], preferred_element_type=F32)
+        x_ref[at, cols] = x_ref[at, cols] + update
 
 
 def ends_kernel(bases_hbm, to_core, to_chip, codes, spread, own, sem):
@@ -109,51 +113,71 @@
     one_hot = one_hot_rows(codes[...], spread[...])
     x_ref[HALO : HALO + SLAB, :] = jnp.dot(one_hot, table[...], preferred_element_type=F32)
     spread_taps(taps, gains, wide_taps)
-    norm_rows(x_ref, n_ref, 0, 112, 368)
+    norm_rows(x_ref, n_ref, 0, 112, 256)
     for layer, low, high in ((0, 128, 352), (1, 144, 336)):
         middle = (low + high) // 2
         for start, stop in ((low, middle), (middle, high)):
-            conv_rows(n_ref, a_ref, layer, wide_taps, start, stop, start - low)
-            mix(a_ref, x_ref, point.at[layer], start, stop, start - low)
-            norm_rows(x_ref, n_ref, layer + 1, start, stop)
-
-
-def outer_kernel(
-    inner, outer, spread, gains, taps, table, point, query_w, key_w, x_in, n_in,
-    trunk_out, keys_out, query_out, x_ref, n_ref, wide_taps, a_ref,
+            conv_rows(n_ref, a_ref, layer, wide_taps, start, stop - start, start - low)
+            mix(a_ref, x_ref, point.at[layer], start, stop - start, start - low)
+            norm_rows(x_ref, n_ref, layer + 1, start, stop - start)
+
+
+def side_base(far, low, high):
+    core = lax.axis_index("core")
+    return pl.multiple_of(jnp.where((core == 0) == far, low, high), STEP)
+
+
+def near_kernel(
+    codes, spread, wide_taps, table, point, x_in, n_in,
+    x_ref, n_ref, a_ref,
+):
+    del x_in, n_in
+    one_hot = one_hot_rows(codes[...], spread[...])
+    base = side_base(False, 0, 368)
+    x_ref[rows_at(base, 0, HALO), :] = jnp.dot(one_hot, table[...], preferred_element_type=F32)
+    norm_rows(x_ref, n_ref, 0, base, HALO)
+    base = side_base(False, 16, 352)
+    conv_rows(n_ref, a_ref, 0, wide_taps, base, HALO, 0)
+    mix(a_ref, x_ref, point.at[0], base, HALO, 0)
+    norm_rows(x_ref, n_ref, 1, base, HALO)
+    conv_rows(n_ref, a_ref, 2, wide_taps, 208, 64, HALO)
+    base = side_base(False, 32, 336)
+    conv_rows(n_ref, a_ref, 1, wide_taps, base, HALO, 0)
+    mix(a_ref, x_ref, point.at[1], base, HALO, 0)
+    norm_rows(x_ref, n_ref, 2, base, HALO)
+    base = side_base(False, 96, 272)
+    conv_rows(n_ref, a_ref, 2, wide_taps, base, HALO, 0)
+    mix(a_ref, x_ref, point.at[2], base, HALO, 0)
+    mix(a_ref, x_ref, point.at[2], 208, 64, HALO)
+
+
+def far_kernel(
+    codes, spread, wide_taps, table, point, query_w, key_w, x_in, n_in,
+    trunk_out, keys_out, query_out, x_ref, n_ref, a_ref,
 ):
     del x_in, n_in
     place = lax.axis_index(("x_hi", "z", "core"))
     core = lax.axis_index("core")
-    low_bases = jnp.where(core == 0, outer[...], inner[...])
-    high_bases = jnp.where(core == 0, inner[...], outer[...])
-    a_ref[0:HALO, 0 : 4 * BASES] = one_hot_rows(low_bases, spread[...])
-    a_ref[HALO : 2 * HALO, 0 : 4 * BASES] = one_hot_rows(high_bases, spread[...])
-    x_ref[0:HALO, :] = jnp.dot(
-        a_ref[0:HALO, 0 : 4 * BASES], table[...], preferred_element_type=F32
-    )
-    x_ref[HALO + SLAB :, :] = jnp.dot(
-        a_ref[HALO : 2 * HALO, 0 : 4 * BASES], table[...], preferred_element_type=F32
-    )
-    spread_taps(taps, gains, wide_taps)
-    low_scale = jnp.where(place == 0, 0.0, 1.0)
-    high_scale = jnp.where(place == 31, 0.0, 1.0)
-
-    norm_rows(x_ref, n_ref, 0, 0, 112, low_scale)
-    norm_rows(x_ref, n_ref, 0, 368, 480, high_scale)
-    for layer, reach_out in ((0, 0), (1, 16)):
-        low, high = 16 + reach_out, 352 - reach_out
-        conv_rows(n_ref, a_ref, layer, wide_taps, low, low + 112, 0)
-        mix(a_ref, x_ref, point.at[layer], low, low + 112, 0)
-        norm_rows(x_ref, n_ref, layer + 1, low, 112, low_scale)
-        norm_rows(x_ref, n_ref, layer + 1, 112, low + 112)
-        conv_rows(n_ref, a_ref, layer, wide_taps, high, high + 112, 112)
-        mix(a_ref, x_ref, point.at[layer], high, high + 112, 112)
-        norm_rows(x_ref, n_ref, layer + 1, high, 368)
-        norm_rows(x_ref, n_ref, layer + 1, 368, high + 112, high_scale)
-    for start, stop in ((96, 240), (240, 384)):
-        conv_rows(n_ref, a_ref, 2, wide_taps, start, stop, start - 96)
-        mix(a_ref, x_ref, point.at[2], start, stop, start - 96)
+    one_hot = one_hot_rows(codes[...], spread[...])
+    base = side_base(True, 0, 368)
+    x_ref[rows_at(base, 0, HALO), :] = jnp.dot(one_hot, table[...], preferred_element_type=F32)
+    beyond = (place == 0) | (place == 31)
+    gone = jnp.where(beyond, 0.0, 1.0)
+    gone_low = jnp.where(beyond & (core == 0), 0.0, 1.0)
+    gone_high = jnp.where(beyond & (core == 1), 0.0, 1.0)
+
+    norm_rows(x_ref, n_ref, 0, base, HALO, [gone] * 7)
+    base = side_base(True, 16, 352)
+    conv_rows(n_ref, a_ref, 0, wide_taps, base, HALO, 0)
+    mix(a_ref, x_ref, point.at[0], base, HALO, 0)
+    norm_rows(x_ref, n_ref, 1, base, HALO, [gone_low] + [gone] * 5 + [gone_high])
+    base = side_base(True, 32, 336)
+    conv_rows(n_ref, a_ref, 1, wide_taps, base, HALO, 0)
+    mix(a_ref, x_ref, point.at[1], base, HALO, 0)
+    norm_rows(x_ref, n_ref, 2, base, HALO, [gone_low] * 2 + [gone] * 3 + [gone_high] * 2)
+    base = side_base(True, 96, 272)
+    conv_rows(n_ref, a_ref, 2, wide_taps, base, HALO, 0)
+    mix(a_ref, x_ref, point.at[2], base, HALO, 0)
 
     trunk = x_ref[96:384, :].astype(BF16)
     trunk_out[...] = trunk[POOL : POOL + SLAB, :]
@@ -272,37 +296,50 @@
         jax.ShapeDtypeStruct((ROWS, C), F32),
         jax.ShapeDtypeStruct((3, C // 128, ROWS, 128), F32),
     )
-    x, n = pl.pallas_call(
+    x, n, wide_taps = pl.pallas_call(
         inner_kernel,
-        out_shape=state,
+        out_shape=state + (jax.ShapeDtypeStruct((3, 5, 8, C), F32),),
         in_specs=vmem(6),
-        out_specs=tuple(vmem(2)),
-        scratch_shapes=[pltpu.VMEM((3, 5, 8, C), F32), pltpu.VMEM((SLAB, C), BF16)],
+        out_specs=tuple(vmem(3)),
+        scratch_shapes=[pltpu.VMEM((SLAB, C), BF16)],
         compiler_params=pltpu.CompilerParams(vmem_limit_bytes=12 * 1024 * 1024),
         cost_estimate=pl.CostEstimate(
             flops=800_000_000, bytes_accessed=5_000_000, transcendentals=400_000
         ),
         name="inner",
     )(codes, spread, embed_table, norm_gains, taps, point_weight)
+    x, n = pl.pallas_call(
+        near_kernel,
+        out_shape=state,
+        in_specs=vmem(7),
+        out_specs=tuple(vmem(2)),
+        scratch_shapes=[pltpu.VMEM((288, C), BF16)],
+        input_output_aliases={5: 0, 6: 1},
+        compiler_params=pltpu.CompilerParams(vmem_limit_bytes=12 * 1024 * 1024),
+        cost_estimate=pl.CostEstimate(
+            flops=600_000_000, bytes_accessed=1_000_000, transcendentals=300_000
+        ),
+        name="near",
+    )(inner, spread, wide_taps, embed_table, point_weight, x, n)
     trunk, keys, queries, _, _ = pl.pallas_call(
-        outer_kernel,
+        far_kernel,
         out_shape=(
             jax.ShapeDtypeStruct((SLAB, C), BF16),
             jax.ShapeDtypeStruct((16, 16, PC), BF16),
             jax.ShapeDtypeStruct((32, PC), F32),
         )
         + state,
-        in_specs=vmem(11),
+        in_specs=vmem(9),
         out_specs=tuple(vmem(5)),
-        scratch_shapes=[pltpu.VMEM((3, 5, 8, C), F32), pltpu.VMEM((288, C), BF16)],
-        input_output_aliases={9: 3, 10: 4},
-        compiler_params=pltpu.CompilerParams(vmem_limit_bytes=16 * 1024 * 1024),
-        cost_estimate=pl.CostEstimate(
-            flops=1_000_000_000, bytes_accessed=1_000_000, transcendentals=600_000
-        ),
-        name="outer",
+        scratch_shapes=[pltpu.VMEM((288, C), BF16)],
+        input_output_aliases={7: 3, 8: 4},
+        compiler_params=pltpu.CompilerParams(vmem_limit_bytes=12 * 1024 * 1024),
+        cost_estimate=pl.CostEstimate(
+            flops=600_000_000, bytes_accessed=1_000_000, transcendentals=300_000
+        ),
+        name="far",
     )(
-        inner, outer, spread, norm_gains, taps, embed_table, point_weight, query_weight, key_weight, x, n
+        outer, spread, wide_taps, embed_table, point_weight, query_weight, key_weight, x, n
     )
 
     own_keys = lax.all_to_all(keys, ("x_hi", "z"), 0, 0, tiled=False)

time: 37.4 us -> 38.3 us (1.024)
  Pallas kernels: 9.75 us -> 11.8 us
  waiting for transfers between devices: 1 us -> 0.01 us
  starting transfers between devices: 8.01 us -> 7.05 us
  blocking collectives: 17.7 us -> 18.5 us
    ppermute x1, starting transfers between devices: 3.29 us -> 0.09 us  [on_device(): inner = lax.ppermute(to_core, 'core', [(0, 1), (1, 0)])]
    ppermute x1, starting transfers between devices: 1.91 us -> 5.06 us  [on_device(): outer = lax.ppermute(to_chip, seq, outer_pairs)]
    pallas_call x2 -> x3, Pallas kernels: 5.39 us -> 7.42 us  [the longest x1 2.83 us: on_device(): pl.pallas_call(far_kernel, out_shape=(jax.ShapeDtypeStruct((SLAB, C), BF1...]
    ppermute x1, waiting for transfers between devices: 0.99 us -> 0.01 us  [on_device(): outer = lax.ppermute(to_chip, seq, outer_pairs)]
    ppermute x1, starting transfers between devices: 2.81 us -> 1.9 us  [on_device(): other_keys = lax.ppermute(own_keys, 'core', [(0, 1), (1, 0)])]
    all_to_all x1, blocking collectives: 17.7 us -> 18.5 us  [on_device(): own_keys = lax.all_to_all(keys, ('x_hi', 'z'), 0, 0, tiled=False)]
  transfers between devices with their start and end apart: 3 -> 3, of which waited for: 1 -> 0; matrix products, arithmetic and copies ran while one was open for 0% -> 0% of each run, Pallas kernels for 9% -> 15%
where the time goes in v7:
time: 38.3 us; the launch traced here: 38.2 us
  blocking collectives  18.5 us (48%)
  Pallas kernels  11.8 us (31%)
  starting transfers between devices  7.05 us (18%)
  between operations  0.81 us (2%)
    all_to_all x1, blocking collectives, on_device(): own_keys = lax.all_to_all(keys, ('x_hi', 'z'), 0, 0, tiled=False)  18.5 us
    ppermute x1, starting transfers between devices, on_device(): outer = lax.ppermute(to_chip, seq, outer_pairs)  5.06 us
    pallas_call x1, Pallas kernels, on_device(): pl.pallas_call(far_kernel, out_shape=(jax.ShapeDtypeStruct((SLAB, C), BF1...  2.83 us
    pallas_call x1, Pallas kernels, on_device(): pl.pallas_call(near_kernel, out_shape=state, in_specs=vmem(7), out_specs=...  2.42 us
    pallas_call x1, Pallas kernels, on_device(): pl.pallas_call(inner_kernel, out_shape=state + (jax.ShapeDtypeStruct((3,...  2.17 us
    pallas_call x1, Pallas kernels, on_device(): pl.pallas_call(pair_kernel_body, out_shape=jax.ShapeDtypeStruct((16, 512,...  2.14 us
    ppermute x1, starting transfers between devices, on_device(): other_keys = lax.ppermute(own_keys, 'core', [(0, 1), (1, 0)])  1.9 us
    pallas_call x1, Pallas kernels, on_device(): pl.pallas_call(weights_kernel, out_shape=(jax.ShapeDtypeStruct((8, 3 * PC...  1.13 us
  transfers between devices with their start and end apart: 3, of which 0 were waited for; matrix products, arithmetic and copies ran while one was open for 0% of the time, Pallas kernels for 15%

profile of v7, /device:TPU:1, one launch (start us, length us, event | category | flops | bytes accessed | tf_op | source)
XLA Modules:
  0.0 38.2 jit_solution(15228281759614124)
XLA Ops:
  0.6 0.0 copy-start
  0.6 0.0 copy-start.1
  0.7 0.0 copy-start.4
  0.7 0.0 copy-start.5
  0.7 1.1 %ends.1 = (bf16[112,128]{1,0:T(8,128)(2,1)S(1)}, bf16[112,128]{1,0:T(8,128)(2,1)S(1)}, bf16[256,128]{1,0:T(8,128)(2,1)S(1)}, bf16[128,512]{1,0:T(8,128)(2,1)S(1)}) custom-call(s32[256,128]{1,0:T(8,128)} %bases_hbm.1), custom_call_target="tpu_custom_call" | custom-call | flops 20000000000 | bytes 1000000 | tf_op jit(solution)/shard_map/ends/pallas_call | solution.py:274
  1.8 5.1 %collective-permute-start = (bf16[112,128]{1,0:T(8,128)(2,1)S(1)}, bf16[112,128]{1,0:T(8,128)(2,1)S(1)}, u32[]{:S(2)}, u32[]{:S(2)}) collective-permute-start(bf16[112,128]{1,0:T(8,128)(2,1)S(1)} %get-tuple-element.16), channel_id=1, source_target_pairs={{8,16},{16,8},{24,32},{32,24},{40,48},{48,40},{56,64},{64,56},{72,... | collective-permute-start | bytes 86024 | tf_op jit(solution)/shard_map/ppermute | solution.py:292
  6.8 0.1 collective-permute-start.1
  6.9 0.0 copy-done
  6.9 0.0 copy-done.1
  6.9 0.0 copy-done.4
  7.0 0.0 copy-done.5
  7.0 2.2 %inner.1 = (f32[480,768]{1,0:T(8,128)S(1)}, f32[3,6,480,128]{3,2,1,0:T(8,128)S(1)}, f32[3,5,8,768]{3,2,1,0:T(8,128)S(1)}) custom-call(bf16[256,128]{1,0:T(8,128)(2,1)S(1)} %get-tuple-element.18.codes, bf16[128,512]{1,0:T(8,128)(2,1)S(1)} %get-tuple-element.17.spread, bf16[512,768]{1,0:T(8,128)(2,1)S(1)} %copy-done.1, f32[3,768]{1,0:T(4,128)S(1)} %copy-done.5, ...), custom_call_target="tpu_custom_call" | custom-call | flops 800000000 | bytes 5000000 | tf_op jit(solution)/shard_map/inner/pallas_call | solution.py:299
  9.1 0.0 collective-permute-done.1.codes
  9.2 0.0 copy-start.2
  9.2 0.0 copy-start.3
  9.2 2.4 %near.1 = (f32[480,768]{1,0:T(8,128)S(1)}, f32[3,6,480,128]{3,2,1,0:T(8,128)S(1)}) custom-call(bf16[112,128]{1,0:T(8,128)(2,1)S(1)} %collective-permute-done.1.codes, bf16[128,512]{1,0:T(8,128)(2,1)S(1)} %get-tuple-element.17.spread, f32[3,5,8,768]{3,2,1,0:T(8,128)S(1)} %get-tuple-element.19.wide_taps, ...), custom_call_target="tpu_custom_call", output_to_operand_aliasing={{0}: (5, {}), {1}: (6, {})} | custom-call | flops 600000000 | bytes 1000000 | tf_op jit(solution)/shard_map/near/pallas_call | solution.py:311
  11.6 0.0 collective-permute-done.codes
  11.6 0.0 copy-done.2
  11.6 0.0 copy-done.3
  11.6 0.0 copy-start.6
  11.6 2.8 %far.1 = (bf16[256,768]{1,0:T(8,128)(2,1)S(1)}, bf16[16,16,128]{2,1,0:T(8,128)(2,1)S(1)}, f32[32,128]{1,0:T(8,128)S(1)}, f32[480,768]{1,0:T(8,128)S(1)}, f32[3,6,480,128]{3,2,1,0:T(8,128)S(1)}) custom-call(bf16[112,128]{1,0:T(8,128)(2,1)S(1)} %collective-permute-done.codes, ...), custom_call_target="tpu_custom_call", output_to_operand_aliasing={{3}: (7, {}), {4}: (8, {})} | custom-call | flops 600000000 | bytes 1000000 | tf_op jit(solution)/shard_map/far/pallas_call | solution.py:324
  14.5 18.5 %all_to_all.5.own = bf16[16,16,128]{2,1,0:T(8,128)(2,1)S(1)} all-to-all(bf16[16,16,128]{2,1,0:T(8,128)(2,1)S(1)} %get-tuple-element.28), channel_id=1, replica_groups=mesh['x_hi'=2,'z'=8,'core'=2,'batch'=8] {'x_hi','z'}, dimensions={0} | all-to-all | bytes 131072 | tf_op jit(solution)/shard_map/all_to_all | solution.py:345
  33.0 1.9 %collective-permute-start.2 = (bf16[16,16,128]{2,1,0:T(8,128)(2,1)S(1)}, bf16[16,16,128]{2,1,0:T(8,128)(2,1)S(1)}, u32[]{:S(2)}, u32[]{:S(2)}) collective-permute-start(bf16[16,16,128]{2,1,0:T(8,128)(2,1)S(1)} %all_to_all.5.own), channel_id=1, source_target_pairs={{0,8},{8,0},{1,9},{9,1},{2,10},{10,2},{3,11},{11,3},{4,12},{12,4},... | collective-permute-start | bytes 196616 | tf_op jit(solution)/shard_map/ppermute | solution.py:346
  34.9 0.0 copy-done.6
  34.9 1.1 %weights.1 = (bf16[8,384,256]{2,1,0:T(8,128)(2,1)S(1)}, bf16[256,768]{1,0:T(8,128)(2,1)}) custom-call(f32[32,128]{1,0:T(8,128)S(1)} %get-tuple-element.25.queries, bf16[3,3,128,128]{3,2,1,0:T(8,128)(2,1)S(1)} %copy-done.6, bf16[256,768]{1,0:T(8,128)(2,1)S(1)} %get-tuple-element.26.trunk), custom_call_target="tpu_custom_call" | custom-call | flops 400000000 | bytes 2000000 | tf_op jit(solution)/shard_map/weights/pallas_call | solution.py:348
  36.1 0.0 collective-permute-done.2.other
  36.1 2.1 %pair.1 = bf16[16,512,128]{2,1,0:T(8,128)(2,1)} custom-call(f32[32,128]{1,0:T(8,128)S(1)} %get-tuple-element.25.queries, bf16[16,16,128]{2,1,0:T(8,128)(2,1)S(1)} %all_to_all.5.own, bf16[16,16,128]{2,1,0:T(8,128)(2,1)S(1)} %collective-permute-done.2.other, bf16[8,384,256]{2,1,0:T(8,128)(2,1)S(1)} %get-tuple-element.29.weights), custom_call_target="tpu_custom_call" | custom-call | tf_op jit(solution)/shard_map/pair/pallas_call | solution.py:363
Async XLA Ops:
  0.6 6.3 %copy-start = (bf16[3,768,768]{2,1,0:T(8,128)(2,1)S(1)}, bf16[3,768,768]{2,1,0:T(8,128)(2,1)}, u32[]{:S(2)}) copy-start(bf16[3,768,768]{2,1,0:T(8,128)(2,1)} %point.5) | copy-start | bytes 10616836
  0.6 6.3 %copy-start.1 = (bf16[512,768]{1,0:T(8,128)(2,1)S(1)}, bf16[512,768]{1,0:T(8,128)(2,1)}, u32[]{:S(2)}) copy-start(bf16[512,768]{1,0:T(8,128)(2,1)} %table.5) | copy-start | bytes 2359300
  0.7 6.3 %copy-start.4 = (f32[3,5,768]{2,0,1:T(4,128)S(1)}, f32[3,5,768]{2,0,1:T(4,128)}, u32[]{:S(2)}) copy-start(f32[3,5,768]{2,0,1:T(4,128)} %param.11) | copy-start | bytes 138244
  0.7 6.3 %copy-start.5 = (f32[3,768]{1,0:T(4,128)S(1)}, f32[3,768]{1,0:T(4,128)}, u32[]{:S(2)}) copy-start(f32[3,768]{1,0:T(4,128)} %gains.1) | copy-start | bytes 27652
  1.8 9.8 %collective-permute-start = (bf16[112,128]{1,0:T(8,128)(2,1)S(1)}, bf16[112,128]{1,0:T(8,128)(2,1)S(1)}, u32[]{:S(2)}, u32[]{:S(2)}) collective-permute-start(bf16[112,128]{1,0:T(8,128)(2,1)S(1)} %get-tuple-element.16), channel_id=1, source_target_pairs={{8,16},{16,8},{24,32},{32,24},{40,48},{48,40},{56,64},{64,56},{72,... | collective-permute-start | bytes 86024 | tf_op jit(solution)/shard_map/ppermute | solution.py:292
  6.8 2.3 %collective-permute-start.1 = (bf16[112,128]{1,0:T(8,128)(2,1)S(1)}, bf16[112,128]{1,0:T(8,128)(2,1)S(1)}, u32[]{:S(2)}, u32[]{:S(2)}) collective-permute-start(bf16[112,128]{1,0:T(8,128)(2,1)S(1)} %get-tuple-element.20), channel_id=1, source_target_pairs={{0,8},{8,0},{1,9},{9,1},{2,10},{10,2},{3,11},{11,3},{4,12},{12,4},... | collective-permute-start | bytes 86024 | tf_op jit(solution)/shard_map/ppermute | solution.py:291
  9.2 2.5 %copy-start.2 = (bf16[768,128]{1,0:T(8,128)(2,1)S(1)}, bf16[768,128]{1,0:T(8,128)(2,1)}, u32[]{:S(2)}) copy-start(bf16[768,128]{1,0:T(8,128)(2,1)} %query_w.1) | copy-start | bytes 589828
  9.2 2.5 %copy-start.3 = (bf16[768,128]{1,0:T(8,128)(2,1)S(1)}, bf16[768,128]{1,0:T(8,128)(2,1)}, u32[]{:S(2)}) copy-start(bf16[768,128]{1,0:T(8,128)(2,1)} %key_w.1) | copy-start | bytes 589828
  11.6 23.3 %copy-start.6 = (bf16[3,3,128,128]{3,2,1,0:T(8,128)(2,1)S(1)}, bf16[3,3,128,128]{3,2,1,0:T(8,128)(2,1)}, u32[]{:S(2)}) copy-start(bf16[3,3,128,128]{3,2,1,0:T(8,128)(2,1)} %kernel.1) | copy-start | bytes 884740
  33.0 3.1 %collective-permute-start.2 = (bf16[16,16,128]{2,1,0:T(8,128)(2,1)S(1)}, bf16[16,16,128]{2,1,0:T(8,128)(2,1)S(1)}, u32[]{:S(2)}, u32[]{:S(2)}) collective-permute-start(bf16[16,16,128]{2,1,0:T(8,128)(2,1)S(1)} %all_to_all.5.own), channel_id=1, source_target_pairs={{0,8},{8,0},{1,9},{9,1},{2,10},{10,2},{3,11},{11,3},{4,12},{12,4},... | collective-permute-start | bytes 196616 | tf_op jit(solution)/shard_map/ppermute | solution.py:346
